TPU v7x, 128 devices: a whole 4x4x4 slice. The times are simulated.
128 devices in a mesh: req: 16 (over x, z), exp: 8 (over y, core).
Axes of the slice: x: 4, y: 4, z: 4, core: 2. Of those that a mesh axis runs over, the one named last changes fastest.
Arguments:
- tokens: bfloat16 [16384, 2048], P('req'), may hold values from -40 to 40
- routes: int32 [16384, 2], P('req'), may hold values from 0 to 7, all different within a row; in each aligned block of 1024 rows (0 to 1023, 1024 to 2047, ...) at most 320 rows name the same one
- lengths: int32 [64], P('req'), may hold values from 1 to 256, 8192 in all
- cached_prefix_length: int32 [64], P('req'), may hold values from 0 to 64, as said below
- prefix_cache_row: int32 [64], replicated, may hold values from 0 to 15, as said below
- adapter_per_request: int32 [64], P('req'), may hold values from 0 to 63
- adapter_storage_slot: int32 [64], replicated, may hold values from 0 to 63, each once
- router_weight: bfloat16 [2048, 8], replicated, may hold values from -0.125 to 0.125
- key_value_weight: bfloat16 [2048, 4096], P('req', 'exp'), may hold values from -0.125 to 0.125
- expert_query_weight: bfloat16 [2048, 8, 2048], P('req', None, 'exp'), may hold values from -0.125 to 0.125
- expert_output_weight: bfloat16 [8, 2048, 2048], P(None, 'exp', 'req'), may hold values from -0.125 to 0.125
- adapter_down_maps: bfloat16 [64, 2048, 16], P('req'), may hold values from -0.125 to 0.125
- adapter_up_maps: bfloat16 [64, 16, 4096], P('req', None, 'exp'), may hold values from -1.5 to 1.5
- prefix_cache_store: bfloat16 [64, 64, 4096], P('req', None, 'exp'), may hold values from -6 to 6
Outputs:
- attention_out: bfloat16 [16384, 2048], P('req', 'exp')
Inputs may be any that keep to these rules, and one draw needn't show every extreme that they name: `routes`: in each aligned block of 1024 rows (one group) no expert is named by more than 320 rows, and one is named by exactly 320. The lengths sum to 8192 and some request has exactly 256. `cached_prefix_length`: exactly 32 requests have no cached prefix; some request has exactly 64. `prefix_cache_row`: request j of a group keeps its cache in slot j of its row; each row holds exactly one cache in each slot, and no row holds two caches of one group. `adapter_storage_slot`: each slot holds one adapter.
All inputs are finite; a program needn't handle non-finite values. No bound on the sum of `lengths` on one device may be relied on, other than what follows from the above.
Results may differ from a plain program's by a relative error of at most 0.017.
The roundings to bfloat16 on the way count: a program that leaves them out, or rounds other values in their place, can miss the bound.
Values may be sent and summed in bfloat16 or wider, within the bound.
No kernel may reach another device: no remote copies, remote signals or barrier semaphores. Data moves between devices by JAX's collectives and lax.ppermute only.
A program may use at most 128 MiB of HBM per device.

v0:
```python
import jax
import jax.numpy as jnp
from jax import lax
from jax.sharding import PartitionSpec as P

HD = 128
NE = 8
TOPK = 2
CAP = 320


adapter_scale = 0.5


def compact(routes):
    route_flat = routes.reshape(-1)
    pair_count = route_flat.shape[0]
    one_hot = (route_flat[:, None] == jnp.arange(NE, dtype=jnp.int32)[None, :]).astype(jnp.int32)
    earlier = jnp.cumsum(one_hot, axis=0) - one_hot
    route_rank = jnp.sum(earlier * one_hot, axis=1)
    slot_table = (
        jnp.zeros((NE, CAP), jnp.int32)
        .at[route_flat, route_rank]
        .set(jnp.arange(pair_count, dtype=jnp.int32))
    )
    return (route_flat, route_rank, slot_table)


def attend(queries, all_keys, cached_prefix_length):
    per_request = queries.shape[1]
    key_span = all_keys.shape[1]
    cached = key_span - per_request
    scores = jnp.einsum(
        "rtjhd,rshd->rhtjs", queries, all_keys[:, :, :, 0, :], preferred_element_type=jnp.float32
    ) * queries.shape[-1] ** (-0.5)
    key_place = jnp.arange(key_span, dtype=jnp.int32)
    query_place = jnp.arange(per_request, dtype=jnp.int32)
    from_cache = key_place[None, :] < cached_prefix_length[:, None]
    from_prompt = (key_place[None, :] >= cached) & (
        key_place[None, :] - cached <= query_place[:, None]
    )
    allowed = jnp.where(
        key_place[None, None, :] < cached, from_cache[:, None, :], from_prompt[None, :, :]
    )
    allowed = allowed[:, None, :, None, :]
    row_max = jnp.max(jnp.where(allowed, scores, -jnp.inf), axis=-1, keepdims=True)
    weights = jnp.where(allowed, jnp.exp(scores - row_max), 0.0)
    probability = (weights / jnp.sum(weights, axis=-1, keepdims=True)).astype(jnp.bfloat16)
    return jnp.einsum(
        "rhtjs,rshd->rtjhd",
        probability,
        all_keys[:, :, :, 1, :],
        preferred_element_type=jnp.float32,
    ).astype(jnp.bfloat16)


def body(
    tokens,
    routes,
    lengths,
    cached_prefix_length,
    prefix_cache_row,
    adapter_per_request,
    adapter_storage_slot,
    router_weight,
    key_value_weight,
    expert_query_weight,
    expert_output_weight,
    adapter_down_maps,
    adapter_up_maps,
    prefix_cache_store,
):
    group_index = lax.axis_index("req")
    num_requests = lengths.shape[0]
    tok_rows = tokens.shape[0]
    per_request = tok_rows // num_requests
    model_width = tokens.shape[1]
    kv_cols = key_value_weight.shape[1]
    query_cols = expert_query_weight.shape[2]
    heads = kv_cols // (2 * HD)
    cached = prefix_cache_store.shape[1]
    route_flat, route_rank, slot_table = compact(routes)
    picked = tokens[slot_table // 2]
    pieces = (
        lax.all_gather(key_value_weight, "req", axis=0, tiled=True),
        lax.all_gather(expert_query_weight, "req", axis=0, tiled=True),
    )
    key_value_segment = jnp.dot(tokens, pieces[0], preferred_element_type=jnp.float32)
    query_run = jnp.einsum("kcd,dkh->kch", picked, pieces[1], preferred_element_type=jnp.float32)
    adapter_hot = (
        adapter_per_request[:, None]
        == jnp.arange(adapter_storage_slot.shape[0], dtype=jnp.int32)[None, :]
    ).astype(jnp.int32)
    wanted = jnp.sum(adapter_hot * adapter_storage_slot[None, :], axis=1)
    pieces = (
        lax.all_gather(adapter_down_maps, "req", axis=0, tiled=True),
        lax.all_gather(adapter_up_maps, "req", axis=0, tiled=True),
    )
    row_count = pieces[0].shape[0]
    matches = (wanted[:, None] == jnp.arange(row_count, dtype=jnp.int32)[None, :]).astype(
        jnp.bfloat16
    )
    down_run = jnp.einsum("rn,ndq->rdq", matches, pieces[0], preferred_element_type=jnp.float32)
    up_run = jnp.einsum("rn,nqc->rqc", matches, pieces[1], preferred_element_type=jnp.float32)
    reduced_rank_state = jnp.einsum(
        "rtd,rdq->rtq",
        tokens.reshape(num_requests, per_request, model_width),
        down_run.astype(jnp.bfloat16),
        preferred_element_type=jnp.float32,
    ).astype(jnp.bfloat16)
    adapter_term = jnp.einsum(
        "mdg,mgy->mdy",
        reduced_rank_state,
        up_run.astype(jnp.bfloat16),
        preferred_element_type=jnp.float32,
    ).reshape(tok_rows, kv_cols)
    fresh_key_value = (key_value_segment + adapter_scale * adapter_term).astype(jnp.bfloat16)
    own_rows = lax.dynamic_slice_in_dim(
        prefix_cache_row, group_index * num_requests, num_requests, 0
    )
    wanted_slot = own_rows * num_requests + jnp.arange(num_requests, dtype=jnp.int32)
    shard_piece = lax.all_gather(prefix_cache_store, "req", axis=0, tiled=True)
    row_count = shard_piece.shape[0]
    matches = (wanted_slot[:, None] == jnp.arange(row_count, dtype=jnp.int32)[None, :]).astype(
        jnp.bfloat16
    )
    stored = jnp.einsum(
        "rn,nsc->rsc", matches, shard_piece, preferred_element_type=jnp.float32
    ).astype(jnp.bfloat16)
    all_keys = jnp.concatenate(
        [stored, fresh_key_value.reshape(num_requests, per_request, kv_cols)], axis=1
    )
    all_keys = all_keys.reshape(num_requests, cached + per_request, heads, 2, HD)
    queries = query_run.astype(jnp.bfloat16)[route_flat, route_rank].reshape(
        num_requests, per_request, TOPK, heads, HD
    )
    attended = attend(queries, all_keys, cached_prefix_length)
    gathered = attended.reshape(TOPK * tok_rows, query_cols)[slot_table]
    logits = jnp.dot(tokens, router_weight, preferred_element_type=jnp.float32)
    route_hot = (routes[:, :, None] == jnp.arange(NE, dtype=jnp.int32)[None, None, :]).astype(
        jnp.float32
    )
    chosen = jnp.sum(route_hot * logits[:, None, :], axis=-1)
    gate_values = jax.nn.sigmoid(chosen - chosen[:, ::-1])
    live_rows = (
        (jnp.arange(per_request, dtype=jnp.int32)[None, :] < lengths[:, None])
        .reshape(tok_rows)
        .astype(jnp.float32)
    )
    shard_piece = lax.all_gather(expert_output_weight, "req", axis=2, tiled=True)
    out_blocks = jnp.einsum(
        "kch,khn->kcn", gathered, shard_piece, preferred_element_type=jnp.float32
    )
    per_pair = out_blocks[route_flat, route_rank].reshape(tok_rows, TOPK, shard_piece.shape[2])
    partial_value = jnp.sum(per_pair * gate_values[:, :, None], axis=1) * live_rows[:, None]
    return lax.psum_scatter(
        partial_value.astype(jnp.bfloat16), "exp", scatter_dimension=1, tiled=True
    )


def solution(mesh):
    return jax.shard_map(
        body,
        mesh=mesh,
        in_specs=(
            P("req", None),
            P("req", None),
            P("req"),
            P("req"),
            P(),
            P("req"),
            P(),
            P(),
            P("req", "exp"),
            P("req", None, "exp"),
            P(None, "exp", "req"),
            P("req", None, None),
            P("req", None, "exp"),
            P("req", None, "exp"),
        ),
        out_specs=P("req", "exp"),
        check_vma=False,
    )
```

profile of v0, /device:TPU:6, one launch (start us, length us, event | category | flops | bytes accessed | tf_op | source)
XLA Modules:
  0.0 522.6 jit_solution(609906091671764247)
XLA Ops:
  6.5 0.7 all-gather.13.cloned.1.call-update
  7.3 0.0 all-gather.7.cloned.1.call-start
  7.3 0.7 all-gather.7.cloned.1.call-update
  8.0 0.0 all-gather.11.cloned.1.call-start
  8.1 0.7 all-gather.11.cloned.1.call-update
  8.8 0.5 all-gather.9.cloned.1.call-update
  9.3 0.0 all-gather.15.cloned.1.call-start
  9.4 1.9 copy.58
  11.3 0.0 all-gather.17.cloned.1.call-start
  11.4 0.5 all-gather.17.cloned.1.call-update
  11.9 0.0 reduce-scatter.2.cloned.1.call-start
  12.0 0.9 copy.55
  12.9 0.3 eq.90
  13.2 0.3 eq.86
  13.4 0.3 reshape.176
  13.8 2.3 reduce-window.6
  16.0 0.3 slice_reduce_fusion
  16.3 0.2 reduce-window.9
  16.5 0.1 add_bitcast_fusion
  16.7 0.1 multiply_reduce_fusion.1
  16.8 0.1 and_reduce_fusion
  16.9 8.1 %scatter_custom_fusion = s32[2560]{0:T(1024)S(1)} fusion(s32[2048]{0:T(1024)S(1)} %broadcast_select_fusion.1, s32[2048]{0:T(1024)S(1)} %iota.56, s32[]{:T(128)} %constant.20.clone.1), kind=kCustom, calls=%fused_computation.75 | custom fusion | bytes 10244
  25.0 0.1 reshape.184
  25.1 0.1 reshape.188
  25.2 0.1 reshape.202
  25.3 22.9 %gather_fusion = bf16[2560,2048]{1,0:T(8,128)(2,1)} fusion(bf16[1024,2048]{1,0:T(8,128)(2,1)} %param.14, s32[3072]{0:T(1024)S(1)} %pad_clamp_fusion.1), kind=kCustom, calls=%fused_computation | custom fusion | bytes 20981760 | tf_op jit(solution)/shard_map/gather | solution.py:83
  48.2 3.5 fusion.60
  51.7 0.4 rev.3
  52.1 0.2 copy.61
  52.4 0.1 convert_bitcast_fusion
  52.5 0.1 iota_add_fusion.1
  52.6 0.2 select_reduce_fusion.2
  52.8 0.1 iota_compare_fusion.4
  52.9 0.2 fusion.32
  53.0 0.3 broadcast_select_fusion
  53.3 1.1 all-gather.13.cloned.1.call-done
  54.4 3.0 convolution_convert_fusion.1
  57.4 50.3 %all-gather.7.cloned.1.call-done = bf16[64,64,512]{2,1,0:T(8,128)(2,1)} async-done(((bf16[4,64,512]{2,1,0:T(8,128)(2,1)}), bf16[64,64,512]{2,1,0:T(8,128)(2,1)}) %all-gather.7.cloned.1.call-update) | async-done | bytes 4194320 | tf_op jit(solution)/shard_map/all_gather | solution.py:122
  107.8 6.7 %fusion.21 = bf16[4,64,512]{2,0,1:T(4,128)(2,1)S(1)} fusion(bf16[64,64,512]{2,1,0:T(8,128)(2,1)} %all-gather.7.cloned.1.call-done, s32[4]{0:T(128)S(1)} %iota_add_fusion.1), kind=kOutput, calls=%fused_computation.29 | convolution fusion | flops 16908544 | bytes 4456464 | tf_op jit(solution)/shard_map/rn,nsc->rsc/dot_general | solution.py:127
  114.5 0.1 concatenate.13
  114.6 46.6 %all-gather.11.cloned.1.call-done = bf16[64,2048,16]{1,2,0:T(8,128)(2,1)} async-done(((bf16[4,2048,16]{1,2,0:T(8,128)(2,1)}), bf16[64,2048,16]{1,2,0:T(8,128)(2,1)}) %all-gather.11.cloned.1.call-update) | async-done | bytes 4194320 | tf_op jit(solution)/shard_map/all_gather | solution.py:96
  161.2 6.7 %fusion.15 = bf16[4,2048,16]{1,0,2:T(4,128)(2,1)S(1)} fusion(bf16[64,2048,16]{1,2,0:T(8,128)(2,1)} %all-gather.11.cloned.1.call-done, s32[4]{0:T(128)S(1)} %select_reduce_fusion.2), kind=kOutput, calls=%fused_computation.22 | convolution fusion | flops 16908544 | bytes 4456464 | tf_op jit(solution)/shard_map/rn,ndq->rdq/dot_general | solution.py:103
  167.9 4.0 convolution_multiply_fusion
  171.9 35.7 %all-gather.9.cloned.1.call-done = bf16[2048,512]{1,0:T(8,128)(2,1)} async-done(((bf16[128,512]{1,0:T(8,128)(2,1)}), bf16[2048,512]{1,0:T(8,128)(2,1)}) %all-gather.9.cloned.1.call-update) | async-done | bytes 2097168 | tf_op jit(solution)/shard_map/all_gather | solution.py:85
  207.5 6.2 %fusion.18 = bf16[1024,512]{1,0:T(8,128)(2,1)} fusion(f32[4,256,512]{2,1,0:T(8,128)S(1)} %convolution_multiply_fusion, bf16[1024,2048]{1,0:T(8,128)(2,1)} %param.14, bf16[2048,512]{1,0:T(8,128)(2,1)} %all-gather.9.cloned.1.call-done), kind=kOutput, calls=%fused_computation.24 | convolution fusion | flops 2148532224 | bytes 9437184 | tf_op jit(solution)/shard_map/dot_general | solution.py:88
  213.8 1.3 concatenate.14
  215.1 0.1 copy_dynamic-update-slice_fusion.1
  215.2 0.3 copy_dynamic-update-slice_fusion
  215.5 64.7 %all-gather.15.cloned.1.call-done = bf16[2048,8,256]{2,0,1:T(8,128)(2,1)} async-done(((bf16[128,8,256]{2,0,1:T(8,128)(2,1)}), bf16[2048,8,256]{2,0,1:T(8,128)(2,1)}) %all-gather.15.cloned.1.call-update) | async-done | bytes 8388624 | tf_op jit(solution)/shard_map/all_gather | solution.py:86
  280.3 9.2 %convolution_convert_fusion = bf16[8,320,256]{2,1,0:T(8,128)(2,1)S(1)} fusion(bf16[8,320,2048]{2,1,0:T(8,128)(2,1)} %bitcast.79, bf16[2048,8,256]{2,0,1:T(8,128)(2,1)} %all-gather.15.cloned.1.call-done), kind=kOutput, calls=%fused_computation.26 | convolution fusion | flops 2685009920 | bytes 20185088 | tf_op jit(solution)/shard_map/kcd,dkh->kch/dot_general | solution.py:89
  289.5 11.1 %gather_fusion.1 = bf16[2048,256]{1,0:T(8,128)(2,1)S(1)} fusion(bf16[8,320,256]{2,1,0:T(8,128)(2,1)S(1)} %convolution_convert_fusion, s32[2048]{0:T(1024)S(1)} %bitcast.76), kind=kCustom, calls=%fused_computation.1 | custom fusion | bytes 2113536 | tf_op jit(solution)/shard_map/gather | solution.py:134
  300.6 0.3 reshape.178
  300.9 6.3 %fusion.54 = (f32[4,2,256,2]{2,3,1,0:T(2,128)S(1)}, f32[4,2,256,2,320]{2,4,3,1,0:T(8,128)}) fusion(pred[4,256,320]{1,2,0:T(8,128)(4,1)S(1)} %broadcast_select_fusion, bf16[4,256,2,2,128]{4,3,2,1,0:T(2,128)(2,1)S(1)} %reshape.178, bf16[4,320,2,2,128]{4,1,2,0,3:T(8,128)(2,1)} %copy-done.2), kind=kOutput, calls=%fused_computation.96 | convolution fusion | flops 678953280 | bytes 9322496 | tf_op jit(solution)/shard_map/sub | solution.py:47
  307.2 3.3 fusion.20
  310.5 0.8 copy.60
  311.3 0.1 copy.98
  311.4 7.6 %gather_fusion.2 = bf16[2560,256]{1,0:T(8,128)(2,1)S(1)} fusion(bf16[2048,256]{1,0:T(8,128)(2,1)S(1)} %bitcast.78, s32[3072]{0:T(1024)S(1)} %pad_clamp_fusion), kind=kCustom, calls=%fused_computation.2 | custom fusion | bytes 2631680 | tf_op jit(solution)/shard_map/gather | solution.py:138
  319.0 41.1 %all-gather.17.cloned.1.call-done = bf16[8,256,2048]{2,1,0:T(8,128)(2,1)} async-done(((bf16[8,256,128]{2,1,0:T(8,128)(2,1)}), bf16[8,256,2048]{2,1,0:T(8,128)(2,1)}) %all-gather.17.cloned.1.call-update) | async-done | bytes 8388624 | tf_op jit(solution)/shard_map/all_gather | solution.py:150
  360.1 12.0 %fusion.59 = f32[8,320,2048]{2,1,0:T(8,128)} fusion(bf16[8,320,256]{2,1,0:T(8,128)(2,1)S(1)} %bitcast.80, bf16[8,256,2048]{2,1,0:T(8,128)(2,1)} %all-gather.17.cloned.1.call-done), kind=kOutput, calls=%fused_computation.97 | convolution fusion | flops 2684354560 | bytes 30670848 | tf_op jit(solution)/shard_map/kch,khn->kcn/dot_general | solution.py:151
  372.1 51.1 %gather_fusion.3 = f32[2048,2048]{1,0:T(8,128)} fusion(f32[8,320,2048]{2,1,0:T(8,128)} %fusion.59, s32[2048]{0:T(1024)S(1)} %bitcast.77), kind=kCustom, calls=%fused_computation.3 | custom fusion | bytes 33570816 | tf_op jit(solution)/shard_map/gather | solution.py:154
  423.1 20.0 %reshape.180 = f32[1024,2,2048]{2,1,0:T(2,128)} reshape(f32[2048,2048]{1,0:T(8,128)} %gather_fusion.3) | data formatting | bytes 33554432 | tf_op jit(solution)/shard_map/reshape | solution.py:154
  443.2 29.1 %multiply_reduce_fusion = f32[1024,2048]{1,0:T(8,128)} fusion(f32[1024,2,2048]{2,1,0:T(2,128)} %reshape.180, f32[1024,2]{1,0:T(8,128)S(1)} %copy.61), kind=kLoop, calls=%fused_computation.6 | loop fusion | flops 6291456 | bytes 25174016 | tf_op jit(solution)/shard_map/reduce_sum | solution.py:155
  472.3 5.8 %multiply_convert_fusion = bf16[1024,2048]{1,0:T(8,128)(2,1)} fusion(f32[1024,2048]{1,0:T(8,128)} %multiply_reduce_fusion, f32[1024]{0:T(1024)S(1)} %bitcast.83), kind=kLoop, calls=%fused_computation.7 | loop fusion | flops 4194304 | bytes 12587008 | tf_op jit(solution)/shard_map/convert_element_type | solution.py:157
  478.1 37.6 %reduce-scatter.2.cloned.1.call-done = bf16[1024,256]{1,0:T(8,128)(2,1)} async-done(((bf16[1024,2048]{1,0:T(8,128)(2,1)}), bf16[1024,256]{1,0:T(8,128)(2,1)}) %reduce-scatter.2.cloned.1.call-update) | async-done | bytes 524304 | tf_op jit(solution)/shard_map/reduce_scatter | solution.py:156
  (42 shorter events, 0.3 us)
Async XLA Ops:
  6.5 41.6 %copy-start = (bf16[2048,8]{0,1:T(8,128)(2,1)S(1)}, bf16[2048,8]{0,1:T(8,128)(2,1)}, u32[]{:S(2)}) copy-start(bf16[2048,8]{0,1:T(8,128)(2,1)} %param.21) | copy-start | bytes 98308
  6.5 10.2 %copy-start.7 = (s32[2]{0:T(128)S(1)}, s32[2]{0:T(128)}, u32[]{:S(2)}) copy-start(s32[2]{0:T(128)} %constant.62) | copy-start | bytes 28
  6.5 10.3 %copy-start.6 = (s32[2]{0:T(128)S(1)}, s32[2]{0:T(128)}, u32[]{:S(2)}) copy-start(s32[2]{0:T(128)} %constant.65) | copy-start | bytes 28
  6.5 47.9 %all-gather.13.cloned.1.call-start = ((), (), s32[]{:S(2)}) async-start(), calls=%async_computation.4 | async-start | bytes 1114112 | tf_op jit(solution)/shard_map/all_gather | solution.py:97
  7.3 100.5 %all-gather.7.cloned.1.call-start = ((), (), s32[]{:S(2)}) async-start(), calls=%async_computation.1 | async-start | bytes 4456448 | tf_op jit(solution)/shard_map/all_gather | solution.py:122
  8.0 153.2 %all-gather.11.cloned.1.call-start = ((), (), s32[]{:S(2)}) async-start(), calls=%async_computation.3 | async-start | bytes 4456448 | tf_op jit(solution)/shard_map/all_gather | solution.py:96
  8.7 198.8 %all-gather.9.cloned.1.call-start = ((), (), s32[]{:S(2)}) async-start(), calls=%async_computation.2 | async-start | bytes 2228224 | tf_op jit(solution)/shard_map/all_gather | solution.py:85
  9.3 271.0 %all-gather.15.cloned.1.call-start = ((), (), s32[]{:S(2)}) async-start(), calls=%async_computation.5 | async-start | bytes 8912896 | tf_op jit(solution)/shard_map/all_gather | solution.py:86
  11.3 348.7 %all-gather.17.cloned.1.call-start = ((), (), s32[]{:S(2)}) async-start(), calls=%async_computation.6 | async-start | bytes 8912896 | tf_op jit(solution)/shard_map/all_gather | solution.py:150
  11.9 503.8 %reduce-scatter.2.cloned.1.call-start = ((), (), s32[]{:S(2)}) async-start(), calls=%async_computation.7 | async-start | bytes 4718592 | tf_op jit(solution)/shard_map/reduce_scatter | solution.py:156
  48.1 3.5 copy-start.4
  48.1 4.2 copy-start.5
  48.1 4.3 copy-start.9
  48.2 4.4 copy-start.10
  48.2 4.4 copy-start.11
  48.2 4.6 copy-start.8
  215.5 64.8 %copy-start.2 = (bf16[4,320,2,2,128]{4,1,2,0,3:T(8,128)(2,1)}, bf16[4,320,2,2,128]{4,1,2,0,3:T(8,128)(2,1)S(1)}, u32[]{:S(2)}) copy-start(bf16[4,320,2,2,128]{4,1,2,0,3:T(8,128)(2,1)S(1)} %copy_dynamic-update-slice_fusion) | copy-start | bytes 3932164
  300.9 6.3 %copy-start.3 = (bf16[4,320,2,2,128]{4,1,2,0,3:T(8,128)(2,1)S(1)}, bf16[4,320,2,2,128]{4,1,2,0,3:T(8,128)(2,1)}, u32[]{:S(2)}) copy-start(bf16[4,320,2,2,128]{4,1,2,0,3:T(8,128)(2,1)} %copy-done.2) | copy-start | bytes 3932164
  472.3 43.4 %copy-start.1 = (bf16[2048,8]{0,1:T(8,128)(2,1)S(1)}, bf16[2048,8]{0,1:T(8,128)(2,1)}, u32[]{:S(2)}) copy-start(bf16[2048,8]{0,1:T(8,128)(2,1)} %param.21) | copy-start | bytes 98308
Sparse Core Ops, SparseCore 0:
  9.5 44.8 all-gather.12
  56.5 51.2 all-gather.6
  109.9 51.2 all-gather.10
  163.2 44.2 all-gather.8
  209.6 70.6 all-gather.14
  282.3 77.7 all-gather.16
  478.3 37.4 reduce-scatter.1
where the time goes:
time: 525 us; the launch traced here: 523 us
  waiting for transfers between devices  280 us (53%)
  local copies, waits for them, and re-layouts  129 us (25%)
  matrix products  60.9 us (12%)
  other arithmetic  38.7 us (7%)
  between operations  13.8 us (3%)
    all_gather x1, waiting for transfers between devices, body(): lax.all_gather(expert_query_weight, 'req', axis=0, tiled=True)  64.7 us
    gather x1, local copies, waits for them, and re-layouts, body(): out_blocks[route_flat, route_rank]  51.1 us
    all_gather x1, waiting for transfers between devices, body(): shard_piece = lax.all_gather(prefix_cache_store, 'req', axis=0, tiled=True)  50.3 us
    all_gather x1, waiting for transfers between devices, body(): lax.all_gather(adapter_down_maps, 'req', axis=0, tiled=True)  46.6 us
    all_gather x1, waiting for transfers between devices, body(): lax.all_gather(expert_output_weight, 'req', axis=2, tiled=True)  41.1 us
    reduce_scatter x1, waiting for transfers between devices, body(): lax.psum_scatter(partial_value.astype(jnp.bfloat16), 'exp', scatter_dimen...  37.6 us
    all_gather x1, waiting for transfers between devices, body(): lax.all_gather(key_value_weight, 'req', axis=0, tiled=True)  35.7 us
    reduce_sum x1, other arithmetic, body(): jnp.sum(per_pair * gate_values[:, :, None], axis=1) * live_rows[:, None]  29.1 us
  transfers between devices with their start and end apart: 7, of which 7 were waited for; matrix products, arithmetic and copies ran while one was open for 21% of the time, Pallas kernels for 0%

commit v1 on v0

v1 whole, which is shorter than its diff:
```python
import jax
import jax.numpy as jnp
from jax import lax
from jax.experimental import pallas as pl
from jax.experimental.pallas import tpu as pltpu
from jax.sharding import PartitionSpec as P

HD = 128
NE = 8
TOPK = 2
SIDE = 4
BF = jnp.bfloat16
F32 = jnp.float32
NEG = -1e30
adapter_scale = 0.5

ROW_Q, ROW_KV, ROW_UP, ROW_DN = 0, 512, 640, 704
SHARD_ROWS = 736
PLACES = []
for _piece, _off in ((0, 0), (1, -1), (2, 1)):
    for _i, _near in enumerate((0, -1, 1, 2)):
        PLACES.append((_piece, _i * SHARD_ROWS, _near, _off))
PLACES += [(3, 0, 0, 2), (3, SHARD_ROWS, -1, 2), (4, 0, 1, 2), (4, SHARD_ROWS, 2, 2)]


def torus(dx, dz):
    return [
        (i, ((i // SIDE + dx) % SIDE) * SIDE + (i % SIDE + dz) % SIDE) for i in range(SIDE * SIDE)
    ]


def send(value, along, step):
    return lax.ppermute(value, "req", torus(step, 0) if along == 0 else torus(0, step))


def ring(value, along):
    before = send(value, along, 1)
    after = send(value, along, -1)
    half = value.shape[0] // 2
    far_low = send(before[:half], along, 1)
    far_high = send(after[half:], along, -1)
    return before, after, far_low, far_high


def source(group, half, first, second):
    x, z = group // SIDE, group % SIDE
    dx, dz = (first, second) if half == 0 else (second, first)
    return ((x + dx + SIDE) % SIDE) * SIDE + (z + dz + SIDE) % SIDE


def pick_rows_kernel(index_ref, store_ref, out_ref, sem):
    copies = []
    for i in range(out_ref.shape[0]):
        copy = pltpu.make_async_copy(store_ref.at[index_ref[i]], out_ref.at[i], sem.at[i])
        copy.start()
        copies.append(copy)
    for copy in copies:
        copy.wait()


def pick_rows(index, store):
    count = index.shape[0]
    return pl.pallas_call(
        pick_rows_kernel,
        out_shape=jax.ShapeDtypeStruct((count,) + store.shape[1:], store.dtype),
        grid_spec=pltpu.PrefetchScalarGridSpec(
            num_scalar_prefetch=1,
            grid=(1,),
            in_specs=[pl.BlockSpec(memory_space=pl.ANY)],
            out_specs=pl.BlockSpec(memory_space=pl.ANY),
            scratch_shapes=[pltpu.SemaphoreType.DMA((count,))],
        ),
        name="pick_rows",
    )(index, store)


def pick_down_kernel(info_ref, *refs):
    pieces, (out_ref, sem) = refs[:10], refs[10:]
    group = info_ref[0]
    for j in range(4):
        slot = info_ref[1 + j]
        owner, inner = slot // 4, slot % 4
        for half in range(2):
            for piece, row, first, second in PLACES:
                here = (owner == source(group, half, first, second)) & (inner // 2 == half)

                @pl.when(here)
                def _(piece=piece, row=row, half=half, j=j, inner=inner):
                    start = pl.multiple_of(row + ROW_DN + (inner % 2) * 16, 16)
                    pltpu.make_async_copy(
                        pieces[half * 5 + piece].at[pl.ds(start, 16), :], out_ref.at[j], sem.at[j]
                    ).start()

    for j in range(4):
        pltpu.make_async_copy(
            pieces[0].at[pl.ds(0, 16), :], out_ref.at[j], sem.at[j]
        ).wait()


def pick_down(info, pieces):
    return pl.pallas_call(
        pick_down_kernel,
        out_shape=jax.ShapeDtypeStruct((4, 16, 256), BF),
        grid_spec=pltpu.PrefetchScalarGridSpec(
            num_scalar_prefetch=1,
            grid=(1,),
            in_specs=[pl.BlockSpec(memory_space=pl.ANY)] * 10,
            out_specs=pl.BlockSpec(memory_space=pl.ANY),
            scratch_shapes=[pltpu.SemaphoreType.DMA((4,))],
        ),
        name="pick_down",
    )(info, *pieces)


def mix_kernel(info_ref, x_ref, routes_ref, down_ref, recv_ref, *refs):
    pieces = refs[:10]
    out_ref = refs[10]
    wq, wkv, up, cache, kv, q, sem_q, sem_kv, sem_up, sem_cache = refs[11:]
    group = info_ref[0]
    for j in range(4):
        pltpu.make_async_copy(recv_ref.at[info_ref[5 + j]], cache.at[j], sem_cache.at[j]).start()
    sources = [
        [source(group, half, first, second) for _, _, first, second in PLACES] for half in range(2)
    ]

    def fetch(row, count, target, sem):
        for half in range(2):
            for at, (piece, base, _, _) in enumerate(PLACES):
                where = pl.multiple_of(sources[half][at] * count, count)
                pltpu.make_async_copy(
                    pieces[half * 5 + piece].at[pl.ds(base + row, count), :],
                    target(half).at[pl.ds(where, count), :],
                    sem(half),
                ).start()

    fetch(ROW_UP, 64, lambda half: up.at[half], lambda half: sem_up.at[half])
    fetch(ROW_KV, 128, lambda half: wkv.at[half], lambda half: sem_kv.at[half])
    for i in range(4):
        fetch(
            ROW_Q + i * 128,
            128,
            lambda half, i=i: wq.at[half * 4 + i],
            lambda half, i=i: sem_q.at[half * 4 + i],
        )
    for half in range(2):
        pltpu.make_async_copy(up.at[half], up.at[half], sem_up.at[half]).wait()
        pltpu.make_async_copy(wkv.at[half], wkv.at[half], sem_kv.at[half]).wait()

    def project_kv(j, carry):
        rows = pl.ds(pl.multiple_of(j * 256, 256), 256)
        x = x_ref[rows, :]
        slot = info_ref[1 + j]
        down = jnp.concatenate([down_ref[e, j] for e in range(NE)], axis=1)
        low = lax.dot_general(x, down, (((1,), (1,)), ((), ())), preferred_element_type=F32).astype(BF)
        for half in range(2):
            base = jnp.dot(x, wkv[half], preferred_element_type=F32)
            lift = up[half, pl.ds(pl.multiple_of(slot * 16, 16), 16), :]
            extra = jnp.dot(low, lift, preferred_element_type=F32)
            kv[half, rows, :] = (base + adapter_scale * extra).astype(BF)
        return carry

    lax.fori_loop(0, 4, project_kv, 0)

    q[...] = jnp.zeros_like(q)

    def project_q(step, carry):
        e = (step % 2) * 4 + step // 2
        pltpu.make_async_copy(wq.at[e], wq.at[e], sem_q.at[e]).wait()
        for j in range(4):
            rows = pl.ds(j * 256, 256)
            value = jnp.dot(x_ref[rows, :], wq[e], preferred_element_type=F32)
            for k in range(TOPK):
                mine = routes_ref[rows, k : k + 1] == e
                q[k, rows, :] = jnp.where(mine, value, q[k, rows, :])
        return carry

    lax.fori_loop(0, NE, project_q, 0)

    for j in range(4):
        pltpu.make_async_copy(recv_ref.at[0], cache.at[j], sem_cache.at[j]).wait()

    def attend(j, carry):
        rows = pl.ds(pl.multiple_of(j * 256, 256), 256)
        cached_length = info_ref[9 + j]
        place = lax.broadcasted_iota(jnp.int32, (512, 320), 1)
        query_at = lax.broadcasted_iota(jnp.int32, (512, 320), 0) % 256
        allowed = ((place < 64) & (place < cached_length)) | (
            (place >= 64) & (place - 64 <= query_at)
        )
        for h in range(2):
            cols = slice(h * HD, (h + 1) * HD)
            keys = jnp.concatenate(
                [cache[j, :, h * 256 : h * 256 + HD], kv[h, rows, 0:HD]], axis=0
            )
            values = jnp.concatenate(
                [cache[j, :, h * 256 + HD : h * 256 + 2 * HD], kv[h, rows, HD : 2 * HD]], axis=0
            )
            queries = jnp.concatenate([q[0, rows, cols], q[1, rows, cols]], axis=0).astype(BF)
            scores = lax.dot_general(
                queries, keys, (((1,), (1,)), ((), ())), preferred_element_type=F32
            ) * (HD**-0.5)
            scores = jnp.where(allowed, scores, NEG)
            weights = jnp.exp(scores - jnp.max(scores, axis=-1, keepdims=True))
            total = jnp.sum(weights, axis=-1, keepdims=True)
            probability = (weights * (1.0 / total)).astype(BF)
            attended = jnp.dot(probability, values, preferred_element_type=F32)
            first, second = attended[:256], attended[256:]
            for e in range(NE):
                chosen = jnp.where(
                    routes_ref[rows, 0:1] == e,
                    first,
                    jnp.where(routes_ref[rows, 1:2] == e, second, 0.0),
                )
                out_ref[e, rows, cols] = chosen.astype(BF)
        return carry

    lax.fori_loop(0, 4, attend, 0)


def mix(info, x, routes, down, recv, pieces):
    any_spec = pl.BlockSpec(memory_space=pl.ANY)
    whole = pl.BlockSpec(memory_space=pltpu.VMEM)
    return pl.pallas_call(
        mix_kernel,
        out_shape=jax.ShapeDtypeStruct((NE, 1024, 256), BF),
        in_specs=[pl.BlockSpec(memory_space=pltpu.SMEM), whole, whole, whole]
        + [any_spec] * 11,
        out_specs=whole,
        scratch_shapes=[
            pltpu.VMEM((NE, 2048, 256), BF),
            pltpu.VMEM((2, 2048, 256), BF),
            pltpu.VMEM((2, 1024, 256), BF),
            pltpu.VMEM((4, 64, 512), BF),
            pltpu.VMEM((2, 1024, 256), BF),
            pltpu.VMEM((TOPK, 1024, 256), F32),
            pltpu.SemaphoreType.DMA((NE,)),
            pltpu.SemaphoreType.DMA((2,)),
            pltpu.SemaphoreType.DMA((2,)),
            pltpu.SemaphoreType.DMA((4,)),
        ],
        compiler_params=pltpu.CompilerParams(vmem_limit_bytes=48 * 2**20),
        name="mix",
    )(info, x, routes, down, recv, *pieces)


def project_out_kernel(gates_ref, lhs_ref, w_ref, out_ref, wide):
    @pl.when(pl.program_id(0) == 0)
    def _():
        for e in range(NE):
            wide[e] = jnp.broadcast_to(gates_ref[:, e : e + 1], (1024, 128))

    def block(i, carry):
        rows = pl.ds(pl.multiple_of(i * 256, 256), 256)
        total = None
        for e in range(NE):
            weight = jnp.concatenate([w_ref[0, e], w_ref[1, e]], axis=1)
            value = jnp.dot(lhs_ref[e, rows, :], weight, preferred_element_type=F32)
            gate = wide[e, rows, :]
            value = value * jnp.concatenate([gate, gate], axis=1)
            total = value if total is None else total + value
        out_ref[rows, :] = total.astype(BF)
        return carry

    lax.fori_loop(0, 4, block, 0)


def project_out(gates, lhs, weight):
    return pl.pallas_call(
        project_out_kernel,
        out_shape=jax.ShapeDtypeStruct((1024, 2048), BF),
        grid=(8,),
        in_specs=[
            pl.BlockSpec((1024, NE), lambda n: (0, 0)),
            pl.BlockSpec((NE, 1024, 256), lambda n: (0, 0, 0)),
            pl.BlockSpec((2, NE, 256, 128), lambda n: (n, 0, 0, 0)),
        ],
        out_specs=pl.BlockSpec((1024, 256), lambda n: (0, n)),
        scratch_shapes=[pltpu.VMEM((NE, 1024, 128), F32)],
        compiler_params=pltpu.CompilerParams(vmem_limit_bytes=40 * 2**20),
        name="project_out",
    )(gates, lhs, weight)


def body(
    tokens,
    routes,
    lengths,
    cached_prefix_length,
    prefix_cache_row,
    adapter_per_request,
    adapter_storage_slot,
    router_weight,
    key_value_weight,
    expert_query_weight,
    expert_output_weight,
    adapter_down_maps,
    adapter_up_maps,
    prefix_cache_store,
):
    group = lax.axis_index("req")
    part = lax.axis_index("exp")
    out_weight = lax.all_gather(expert_output_weight, "req", axis=0, tiled=True).reshape(
        16, NE, 256, 128
    )

    query_rows = expert_query_weight.transpose(1, 0, 2).reshape(NE * 128, 256)
    down_rows = (
        lax.dynamic_slice_in_dim(adapter_down_maps, part * 256, 256, 1)
        .transpose(0, 2, 1)
        .reshape(64, 256)
    )
    up_rows = adapter_up_maps.reshape(64, 512)
    halves = []
    for half in range(2):
        cols = slice(half * 256, half * 256 + 256)
        halves.append(
            jnp.concatenate(
                [
                    query_rows[half * 512 : half * 512 + 512],
                    key_value_weight[:, cols],
                    up_rows[:, cols],
                    down_rows[half * 32 : half * 32 + 32],
                ],
                axis=0,
            )
        )
    near = [jnp.concatenate([halves[half], *ring(halves[half], half)], axis=0) for half in range(2)]
    pieces = []
    for half in range(2):
        pieces += [near[half], *ring(near[half], 1 - half)]

    rows_by_group = prefix_cache_row.reshape(16, 4)
    held = (rows_by_group == group).astype(jnp.int32)
    wanted_by = jnp.sum(held * jnp.arange(4, dtype=jnp.int32)[None, :], axis=1)
    outgoing = pick_rows(wanted_by, prefix_cache_store)
    received = lax.all_to_all(outgoing, "req", split_axis=0, concat_axis=0, tiled=True)

    adapter_hot = (
        adapter_per_request[:, None]
        == jnp.arange(adapter_storage_slot.shape[0], dtype=jnp.int32)[None, :]
    ).astype(jnp.int32)
    slots = jnp.sum(adapter_hot * adapter_storage_slot[None, :], axis=1)
    own_rows = lax.dynamic_slice_in_dim(prefix_cache_row, group * 4, 4, 0)
    info = jnp.concatenate([group[None].astype(jnp.int32), slots, own_rows, cached_prefix_length])

    logits = jnp.dot(tokens, router_weight, preferred_element_type=F32)
    expert = jnp.arange(NE, dtype=jnp.int32)
    route_hot = (routes[:, :, None] == expert[None, None, :]).astype(F32)
    chosen = jnp.sum(route_hot * logits[:, None, :], axis=-1)
    gate_values = jax.nn.sigmoid(chosen - chosen[:, ::-1])
    live = (jnp.arange(256, dtype=jnp.int32)[None, :] < lengths[:, None]).reshape(1024, 1)
    gates = jnp.sum(route_hot * gate_values[:, :, None], axis=1) * live.astype(F32)

    down_part = pick_down(info, pieces)
    down = lax.all_gather(down_part.reshape(1, 4, 16, 256), "exp", axis=0, tiled=True)
    lhs = mix(info, tokens, routes, down, received, pieces)
    partial_value = project_out(gates, lhs, out_weight)
    return lax.psum_scatter(partial_value, "exp", scatter_dimension=1, tiled=True)


def solution(mesh):
    return jax.shard_map(
        body,
        mesh=mesh,
        in_specs=(
            P("req", None),
            P("req", None),
            P("req"),
            P("req"),
            P(),
            P("req"),
            P(),
            P(),
            P("req", "exp"),
            P("req", None, "exp"),
            P(None, "exp", "req"),
            P("req", None, None),
            P("req", None, "exp"),
            P("req", None, "exp"),
        ),
        out_specs=P("req", "exp"),
        check_vma=False,
    )
```

time: 525 us -> 258 us (0.49)
  waiting for transfers between devices: 280 us -> 74.9 us
  local copies, waits for them, and re-layouts: 129 us -> 27 us
  Pallas kernels: 0 us -> 88.9 us
  matrix products: 60.9 us -> 3.48 us
  other arithmetic: 38.7 us -> 3.65 us
  starting transfers between devices: 0.23 us -> 31.4 us
  blocking collectives: 0 us -> 13.8 us
    all_gather x6 -> x1, waiting for transfers between devices: 239 us -> 0.02 us  [body(): lax.all_gather(expert_output_weight, 'req', axis=0, tiled=True)]
    gather x4 -> x0, local copies, waits for them, and re-layouts: 92.6 us -> none  [the longest x1 51.1 us: body(): out_blocks[route_flat, route_rank]]
    pallas_call x0 -> x4, Pallas kernels: none -> 88.9 us  [the longest x1 35 us: mix(): pl.pallas_call(mix_kernel, out_shape=jax.ShapeDtypeStruct((NE, 1024, 256)...]
    dot_general x9 -> x1, matrix products: 54.6 us -> 3.48 us  [body(): logits = jnp.dot(tokens, router_weight, preferred_element_type=F32)]
    ppermute x0 -> x16, waiting for transfers between devices: none -> 35.6 us  [send(): lax.ppermute(value, 'req', torus(step, 0) if along == 0 else torus(0, step))]
    reduce_sum x3, other arithmetic: 29.3 us -> 0.83 us  [the longest x1 0.64 us: body(): wanted_by = jnp.sum(held * jnp.arange(4, dtype=jnp.int32)[None, :], axis=1)]
    ppermute x0 -> x16, starting transfers between devices: none -> 24.6 us  [send(): lax.ppermute(value, 'req', torus(step, 0) if along == 0 else torus(0, step))]
    reshape x3 -> x0, local copies, waits for them, and re-layouts: 20.6 us -> none  [the longest x1 20 us: body(): out_blocks[route_flat, route_rank]]
  transfers between devices with their start and end apart: 7 -> 19, of which waited for: 7 -> 11; matrix products, arithmetic and copies ran while one was open for 21% -> 10% of each run, Pallas kernels for 0% -> 28%
where the time goes in v1:
time: 258 us; the launch traced here: 257 us
  Pallas kernels  88.9 us (34%)
  waiting for transfers between devices  74.9 us (29%)
  starting transfers between devices  31.4 us (12%)
  local copies, waits for them, and re-layouts  27 us (10%)
  blocking collectives  13.8 us (5%)
  between operations  13.7 us (5%)
  other arithmetic  3.65 us (1%)
  matrix products  3.48 us (1%)
    reduce_scatter x1, waiting for transfers between devices, body(): lax.psum_scatter(partial_value, 'exp', scatter_dimension=1, tiled=True)  38.5 us
    ppermute x16, waiting for transfers between devices, send(): lax.ppermute(value, 'req', torus(step, 0) if along == 0 else torus(0, step))  35.6 us
    pallas_call x1, Pallas kernels, mix(): pl.pallas_call(mix_kernel, out_shape=jax.ShapeDtypeStruct((NE, 1024, 256)...  35 us
    pallas_call x1, Pallas kernels, pick_rows(): pl.pallas_call(pick_rows_kernel, out_shape=jax.ShapeDtypeStruct((count,)...  33.8 us
    ppermute x16, starting transfers between devices, send(): lax.ppermute(value, 'req', torus(step, 0) if along == 0 else torus(0, step))  24.6 us
    pallas_call x1, Pallas kernels, project_out(): pl.pallas_call(project_out_kernel, out_shape=jax.ShapeDtypeStruct((1024,...  17.2 us
    unnamed x49, local copies, waits for them, and re-layouts  14.3 us
    all_gather x1, blocking collectives, body(): lax.all_gather(down_part.reshape(1, 4, 16, 256), 'exp', axis=0, tiled=True)  13.8 us
  transfers between devices with their start and end apart: 19, of which 11 were waited for; matrix products, arithmetic and copies ran while one was open for 10% of the time, Pallas kernels for 28%

profile of v1, /device:TPU:6, one launch (start us, length us, event | category | flops | bytes accessed | tf_op | source)
XLA Modules:
  0.0 256.9 jit_solution(9143569720619041143)
XLA Ops:
  6.5 0.7 all-gather.3.cloned.1.call-update
  7.3 1.4 fusion
  8.8 0.9 constant_dynamic-update-slice_fusion.7
  9.7 0.7 fusion.1
  10.4 0.6 fusion.2
  11.0 2.0 collective-permute-start.8
  13.0 2.2 collective-permute-start.9
  15.3 0.5 collective-permute-start
  15.8 1.5 collective-permute-start.1
  17.4 0.6 constant_dynamic-update-slice_fusion.12
  18.0 0.6 constant_dynamic-update-slice_fusion.4
  18.6 5.4 %collective-permute-done.8 = bf16[736,256]{1,0:T(8,128)(2,1)S(1)} collective-permute-done((bf16[736,256]{1,0:T(8,128)(2,1)S(1)}, bf16[736,256]{1,0:T(8,128)(2,1)S(1)}, u32[]{:S(2)}, u32[]{:S(2)}) %collective-permute-start.8) | collective-permute-done | bytes 376864 | tf_op jit(solution)/shard_map/ppermute | solution.py:33
  23.9 0.1 collective-permute-start.10
  24.0 3.3 %collective-permute-start.11 = (bf16[368,256]{1,0:T(8,128)(2,1)S(1)}, bf16[368,256]{1,0:T(8,128)(2,1)S(1)}, u32[]{:S(2)}, u32[]{:S(2)}) collective-permute-start(bf16[368,256]{1,0:T(8,128)(2,1)S(1)} %slice.91), channel_id=1, source_target_pairs={{0,24},{8,0},{16,8},{24,16},{32,56},{40,32},{48,40},{56,48},{64,88... | collective-permute-start | bytes 565256 | tf_op jit(solution)/shard_map/ppermute | solution.py:33
  27.3 1.2 collective-permute-done
  28.5 0.5 collective-permute-start.2
  29.0 3.5 %collective-permute-done.1 = bf16[736,256]{1,0:T(8,128)(2,1)S(1)} collective-permute-done((bf16[736,256]{1,0:T(8,128)(2,1)S(1)}, bf16[736,256]{1,0:T(8,128)(2,1)S(1)}, u32[]{:S(2)}, u32[]{:S(2)}) %collective-permute-start.1) | collective-permute-done | bytes 376864 | tf_op jit(solution)/shard_map/ppermute | solution.py:33
  32.5 0.1 collective-permute-start.3
  32.6 0.8 constant_dynamic-update-slice_fusion.11
  33.4 0.8 constant_dynamic-update-slice_fusion.10
  34.1 0.8 constant_dynamic-update-slice_fusion.3
  34.9 0.8 constant_dynamic-update-slice_fusion.2
  35.7 0.4 collective-permute-done.10
  36.1 0.7 constant_dynamic-update-slice_fusion.9
  36.8 0.7 constant_dynamic-update-slice_fusion.8.refs_5_
  37.5 2.8 %collective-permute-start.12 = (bf16[2944,256]{1,0:T(8,128)(2,1)}, bf16[2944,256]{1,0:T(8,128)(2,1)S(1)}, u32[]{:S(2)}, u32[]{:S(2)}) collective-permute-start(bf16[2944,256]{1,0:T(8,128)(2,1)} %constant_dynamic-update-slice_fusion.8.refs_5_), channel_id=1, source_target_pairs={{0,32},{8,40},{16,48},{24,56},{32,64},{40,72},{48,80},{56,88},{64,... | collective-permute-start | bytes 4521992 | tf_op jit(solution)/shard_map/ppermute | solution.py:33
  40.3 0.7 constant_dynamic-update-slice_fusion.1
  41.0 0.7 constant_dynamic-update-slice_fusion.refs_0_
  41.7 3.2 %collective-permute-start.5 = (bf16[2944,256]{1,0:T(8,128)(2,1)}, bf16[2944,256]{1,0:T(8,128)(2,1)}, u32[]{:S(2)}, u32[]{:S(2)}) collective-permute-start(bf16[2944,256]{1,0:T(8,128)(2,1)} %constant_dynamic-update-slice_fusion.refs_0_), channel_id=1, source_target_pairs={{0,24},{8,0},{16,8},{24,16},{32,56},{40,32},{48,40},{56,48},{64,88... | collective-permute-start | bytes 4521992 | tf_op jit(solution)/shard_map/ppermute | solution.py:33
  44.9 0.1 eq.43
  45.0 0.6 select_reduce_fusion.2.index_ref
  45.6 33.8 %pick_rows.1 = bf16[16,64,512]{2,1,0:T(8,128)(2,1)} custom-call(s32[16]{0:T(128)} %select_reduce_fusion.2.index_ref, bf16[4,64,512]{2,1,0:T(8,128)(2,1)} %store_ref.1), custom_call_target="tpu_custom_call" | custom-call | tf_op jit(solution)/shard_map/pick_rows/pallas_call | solution.py:63
  79.5 6.8 %all-to-all-start = ((bf16[16,64,512]{2,1,0:T(8,128)(2,1)}), bf16[16,64,512]{2,1,0:T(8,128)(2,1)S(1)}, u32[]{:S(2)}, u32[]{:S(2)}) async-start(bf16[16,64,512]{2,1,0:T(8,128)(2,1)} %pick_rows.1), calls=%async_computation | async-start | bytes 2097152 | tf_op jit(solution)/shard_map/all_to_all | solution.py:336
  86.3 3.5 %fusion.4 = f32[1024,8]{0,1:T(8,128)S(1)} fusion(bf16[1024,2048]{1,0:T(8,128)(2,1)} %x_ref.1, bf16[2048,8]{0,1:T(8,128)(2,1)S(1)} %copy-done.13), kind=kOutput, calls=%fused_computation.35 | convolution fusion | flops 33554432 | bytes 4259840 | tf_op jit(solution)/shard_map/dot_general | solution.py:346
  89.8 0.2 rev.3
  90.1 10.7 %collective-permute-done.12.refs_6_ = bf16[2944,256]{1,0:T(8,128)(2,1)S(1)} collective-permute-done((bf16[2944,256]{1,0:T(8,128)(2,1)}, bf16[2944,256]{1,0:T(8,128)(2,1)S(1)}, u32[]{:S(2)}, u32[]{:S(2)}) %collective-permute-start.12) | collective-permute-done | bytes 1507360 | tf_op jit(solution)/shard_map/ppermute | solution.py:33
  100.8 1.2 copy-done.9
  101.9 0.9 slice.92
  102.8 3.6 %collective-permute-start.14 = (bf16[1472,256]{1,0:T(8,128)(2,1)}, bf16[1472,256]{1,0:T(8,128)(2,1)S(1)}, u32[]{:S(2)}, u32[]{:S(2)}) collective-permute-start(bf16[1472,256]{1,0:T(8,128)(2,1)} %slice.92), channel_id=1, source_target_pairs={{0,32},{8,40},{16,48},{24,56},{32,64},{40,72},{48,80},{56,88},{64,... | collective-permute-start | bytes 2261000 | tf_op jit(solution)/shard_map/ppermute | solution.py:33
  106.4 4.1 %collective-permute-done.13.refs_7_ = bf16[2944,256]{1,0:T(8,128)(2,1)} collective-permute-done((bf16[2944,256]{1,0:T(8,128)(2,1)}, bf16[2944,256]{1,0:T(8,128)(2,1)}, u32[]{:S(2)}, u32[]{:S(2)}) %collective-permute-start.13) | collective-permute-done | bytes 1507360 | tf_op jit(solution)/shard_map/ppermute | solution.py:33
  110.6 2.0 slice.93
  112.6 1.8 collective-permute-done.4.refs_1_
  114.4 2.0 slice.85
  116.5 0.1 collective-permute-start.6
  116.6 2.1 slice.86
  118.6 4.7 %collective-permute-start.7 = (bf16[1472,256]{1,0:T(8,128)(2,1)}, bf16[1472,256]{1,0:T(8,128)(2,1)}, u32[]{:S(2)}, u32[]{:S(2)}) collective-permute-start(bf16[1472,256]{1,0:T(8,128)(2,1)} %slice.86), channel_id=1, source_target_pairs={{0,24},{8,0},{16,8},{24,16},{32,56},{40,32},{48,40},{56,48},{64,88... | collective-permute-start | bytes 2261000 | tf_op jit(solution)/shard_map/ppermute | solution.py:33
  123.4 0.2 copy.38.routes_ref
  123.6 0.1 dynamic_slice.6
  123.7 1.0 copy.34
  124.7 0.2 select_reduce_fusion.3
  124.9 0.6 pad_add_fusion.info_ref
  125.5 2.0 broadcast_multiply_fusion.gates_ref
  127.6 4.3 %collective-permute-done.14.refs_8_ = bf16[1472,256]{1,0:T(8,128)(2,1)S(1)} collective-permute-done((bf16[1472,256]{1,0:T(8,128)(2,1)}, bf16[1472,256]{1,0:T(8,128)(2,1)S(1)}, u32[]{:S(2)}, u32[]{:S(2)}) %collective-permute-start.14) | collective-permute-done | bytes 753696 | tf_op jit(solution)/shard_map/ppermute | solution.py:33
  131.9 1.3 collective-permute-done.15.refs_9_
  133.2 2.9 %collective-permute-done.6.refs_3_ = bf16[1472,256]{1,0:T(8,128)(2,1)} collective-permute-done((bf16[1472,256]{1,0:T(8,128)(2,1)}, bf16[1472,256]{1,0:T(8,128)(2,1)}, u32[]{:S(2)}, u32[]{:S(2)}) %collective-permute-start.6) | collective-permute-done | bytes 753696 | tf_op jit(solution)/shard_map/ppermute | solution.py:33
  136.1 2.9 %pick_down.1 = bf16[4,16,256]{2,1,0:T(8,128)(2,1)} custom-call(s32[13]{0:T(128)} %pad_add_fusion.info_ref, bf16[2944,256]{1,0:T(8,128)(2,1)} %constant_dynamic-update-slice_fusion.refs_0_, bf16[2944,256]{1,0:T(8,128)(2,1)} %collective-permute-done.4.refs_1_, bf16[2944,256]{1,0:T(8,128)(2,1)} %collective-permute-done.5.refs_2_, ...), custom_call_target="tpu_custom_call" | custom-call | tf_op jit(solution)/shard_map/pick_down/pallas_call | solution.py:101
  138.9 13.8 %all-gather = bf16[32,16,256]{2,1,0:T(8,128)(2,1)S(1)} all-gather(bf16[4,16,256]{2,1,0:T(8,128)(2,1)} %pick_down.1), channel_id=2, replica_groups=mesh['req'=16,'exp'=8] {'exp'}, dimensions={0}, use_global_device_ids=true | all-gather | bytes 294912 | tf_op jit(solution)/shard_map/all_gather | solution.py:355
  152.8 1.1 copy-done.4
  153.9 1.1 copy-done.6
  155.0 35.0 %mix.1.lhs_ref = bf16[8,1024,256]{2,1,0:T(8,128)(2,1)} custom-call(s32[13]{0:T(128)S(1)} %copy-done.8, bf16[1024,2048]{1,0:T(8,128)(2,1)} %x_ref.1, s32[1024,2]{1,0:T(8,128)S(1)} %copy.38.routes_ref, bf16[8,4,16,256]{3,2,1,0:T(8,128)(2,1)S(1)} %bitcast.16, bf16[16,64,512]{2,1,0:T(8,128)(2,1)S(1)} %all-to-all-done.recv_ref, ...), custom_call_target="tpu_custom_call" | custom-call | tf_op jit(solution)/shard_map/mix/pallas_call | solution.py:223
  190.1 2.2 copy-done.1
  192.3 17.2 %project_out.1 = bf16[1024,2048]{1,0:T(8,128)(2,1)S(1)} custom-call(f32[1024,8]{1,0:T(8,128)S(1)} %copy-done.7, bf16[8,1024,256]{2,1,0:T(8,128)(2,1)S(1)} %copy-done.1, bf16[16,8,256,128]{3,2,1,0:T(8,128)(2,1)} %bitcast.17), custom_call_target="tpu_custom_call" | custom-call | tf_op jit(solution)/shard_map/project_out/pallas_call | solution.py:268
  209.5 1.9 copy-done.2
  211.5 38.5 %reduce-scatter.2.cloned.1.call-done = bf16[1024,256]{1,0:T(8,128)(2,1)} async-done(((bf16[1024,2048]{1,0:T(8,128)(2,1)}), bf16[1024,256]{1,0:T(8,128)(2,1)}) %reduce-scatter.2.cloned.1.call-update) | async-done | bytes 524304 | tf_op jit(solution)/shard_map/reduce_scatter | solution.py:358
  (63 shorter events, 0.5 us)
Async XLA Ops:
  6.5 2.3 copy-start
  6.5 183.5 %all-gather.3.cloned.1.call-start = ((), (), s32[]{:S(2)}) async-start(), calls=%async_computation.2 | async-start | bytes 8912896 | tf_op jit(solution)/shard_map/all_gather | solution.py:302
  7.3 2.4 copy-start.10
  8.7 1.7 copy-start.12
  11.0 12.9 %collective-permute-start.8 = (bf16[736,256]{1,0:T(8,128)(2,1)S(1)}, bf16[736,256]{1,0:T(8,128)(2,1)S(1)}, u32[]{:S(2)}, u32[]{:S(2)}) collective-permute-start(bf16[736,256]{1,0:T(8,128)(2,1)S(1)} %pad_maximum_fusion.1), channel_id=1, source_target_pairs={{0,8},{8,16},{16,24},{24,0},{32,40},{40,48},{48,56},{56,32},{64,72... | collective-permute-start | bytes 1130504 | tf_op jit(solution)/shard_map/ppermute | solution.py:33
  13.0 11.0 %collective-permute-start.9 = (bf16[736,256]{1,0:T(8,128)(2,1)S(1)}, bf16[736,256]{1,0:T(8,128)(2,1)S(1)}, u32[]{:S(2)}, u32[]{:S(2)}) collective-permute-start(bf16[736,256]{1,0:T(8,128)(2,1)S(1)} %pad_maximum_fusion.1), channel_id=1, source_target_pairs={{0,24},{8,0},{16,8},{24,16},{32,56},{40,32},{48,40},{56,48},{64,88... | collective-permute-start | bytes 1130504 | tf_op jit(solution)/shard_map/ppermute | solution.py:33
  15.3 13.2 %collective-permute-start = (bf16[736,256]{1,0:T(8,128)(2,1)S(1)}, bf16[736,256]{1,0:T(8,128)(2,1)S(1)}, u32[]{:S(2)}, u32[]{:S(2)}) collective-permute-start(bf16[736,256]{1,0:T(8,128)(2,1)S(1)} %pad_maximum_fusion), channel_id=1, source_target_pairs={{0,32},{8,40},{16,48},{24,56},{32,64},{40,72},{48,80},{56,88},{64,... | collective-permute-start | bytes 1130504 | tf_op jit(solution)/shard_map/ppermute | solution.py:33
  15.8 16.7 %collective-permute-start.1 = (bf16[736,256]{1,0:T(8,128)(2,1)S(1)}, bf16[736,256]{1,0:T(8,128)(2,1)S(1)}, u32[]{:S(2)}, u32[]{:S(2)}) collective-permute-start(bf16[736,256]{1,0:T(8,128)(2,1)S(1)} %pad_maximum_fusion), channel_id=1, source_target_pairs={{0,96},{8,104},{16,112},{24,120},{32,0},{40,8},{48,16},{56,24},{64... | collective-permute-start | bytes 1130504 | tf_op jit(solution)/shard_map/ppermute | solution.py:33
  23.9 12.2 %collective-permute-start.10 = (bf16[368,256]{1,0:T(8,128)(2,1)S(1)}, bf16[368,256]{1,0:T(8,128)(2,1)S(1)}, u32[]{:S(2)}, u32[]{:S(2)}) collective-permute-start(bf16[368,256]{1,0:T(8,128)(2,1)S(1)} %slice.90), channel_id=1, source_target_pairs={{0,8},{8,16},{16,24},{24,0},{32,40},{40,48},{48,56},{56,32},{64,72... | collective-permute-start | bytes 565256 | tf_op jit(solution)/shard_map/ppermute | solution.py:33
  24.0 12.8 %collective-permute-start.11 = (bf16[368,256]{1,0:T(8,128)(2,1)S(1)}, bf16[368,256]{1,0:T(8,128)(2,1)S(1)}, u32[]{:S(2)}, u32[]{:S(2)}) collective-permute-start(bf16[368,256]{1,0:T(8,128)(2,1)S(1)} %slice.91), channel_id=1, source_target_pairs={{0,24},{8,0},{16,8},{24,16},{32,56},{40,32},{48,40},{56,48},{64,88... | collective-permute-start | bytes 565256 | tf_op jit(solution)/shard_map/ppermute | solution.py:33
  28.5 11.8 %collective-permute-start.2 = (bf16[368,256]{1,0:T(8,128)(2,1)S(1)}, bf16[368,256]{1,0:T(8,128)(2,1)S(1)}, u32[]{:S(2)}, u32[]{:S(2)}) collective-permute-start(bf16[368,256]{1,0:T(8,128)(2,1)S(1)} %slice.83), channel_id=1, source_target_pairs={{0,32},{8,40},{16,48},{24,56},{32,64},{40,72},{48,80},{56,88},{64,... | collective-permute-start | bytes 565256 | tf_op jit(solution)/shard_map/ppermute | solution.py:33
  32.5 8.5 %collective-permute-start.3 = (bf16[368,256]{1,0:T(8,128)(2,1)S(1)}, bf16[368,256]{1,0:T(8,128)(2,1)S(1)}, u32[]{:S(2)}, u32[]{:S(2)}) collective-permute-start(bf16[368,256]{1,0:T(8,128)(2,1)S(1)} %slice.84), channel_id=1, source_target_pairs={{0,96},{8,104},{16,112},{24,120},{32,0},{40,8},{48,16},{56,24},{64... | collective-permute-start | bytes 565256 | tf_op jit(solution)/shard_map/ppermute | solution.py:33
  34.1 10.8 %copy-start.16 = (s32[64]{0:T(128)S(1)}, s32[64]{0:T(128)}, u32[]{:S(2)}) copy-start(s32[64]{0:T(128)} %param.18) | copy-start | bytes 772
  37.5 63.3 %collective-permute-start.12 = (bf16[2944,256]{1,0:T(8,128)(2,1)}, bf16[2944,256]{1,0:T(8,128)(2,1)S(1)}, u32[]{:S(2)}, u32[]{:S(2)}) collective-permute-start(bf16[2944,256]{1,0:T(8,128)(2,1)} %constant_dynamic-update-slice_fusion.8.refs_5_), channel_id=1, source_target_pairs={{0,32},{8,40},{16,48},{24,56},{32,64},{40,72},{48,80},{56,88},{64,... | collective-permute-start | bytes 4521992 | tf_op jit(solution)/shard_map/ppermute | solution.py:33
  40.3 70.3 %collective-permute-start.13 = (bf16[2944,256]{1,0:T(8,128)(2,1)}, bf16[2944,256]{1,0:T(8,128)(2,1)}, u32[]{:S(2)}, u32[]{:S(2)}) collective-permute-start(bf16[2944,256]{1,0:T(8,128)(2,1)} %constant_dynamic-update-slice_fusion.8.refs_5_), channel_id=1, source_target_pairs={{0,96},{8,104},{16,112},{24,120},{32,0},{40,8},{48,16},{56,24},{64... | collective-permute-start | bytes 4521992 | tf_op jit(solution)/shard_map/ppermute | solution.py:33
  41.7 72.8 %collective-permute-start.4 = (bf16[2944,256]{1,0:T(8,128)(2,1)}, bf16[2944,256]{1,0:T(8,128)(2,1)}, u32[]{:S(2)}, u32[]{:S(2)}) collective-permute-start(bf16[2944,256]{1,0:T(8,128)(2,1)} %constant_dynamic-update-slice_fusion.refs_0_), channel_id=1, source_target_pairs={{0,8},{8,16},{16,24},{24,0},{32,40},{40,48},{48,56},{56,32},{64,72... | collective-permute-start | bytes 4521992 | tf_op jit(solution)/shard_map/ppermute | solution.py:33
  41.7 74.9 %collective-permute-start.5 = (bf16[2944,256]{1,0:T(8,128)(2,1)}, bf16[2944,256]{1,0:T(8,128)(2,1)}, u32[]{:S(2)}, u32[]{:S(2)}) collective-permute-start(bf16[2944,256]{1,0:T(8,128)(2,1)} %constant_dynamic-update-slice_fusion.refs_0_), channel_id=1, source_target_pairs={{0,24},{8,0},{16,8},{24,16},{32,56},{40,32},{48,40},{56,48},{64,88... | collective-permute-start | bytes 4521992 | tf_op jit(solution)/shard_map/ppermute | solution.py:33
  45.6 40.6 %copy-start.13 = (bf16[2048,8]{0,1:T(8,128)(2,1)S(1)}, bf16[2048,8]{0,1:T(8,128)(2,1)}, u32[]{:S(2)}) copy-start(bf16[2048,8]{0,1:T(8,128)(2,1)} %param.21) | copy-start | bytes 98308
  79.5 73.3 %all-to-all-start = ((bf16[16,64,512]{2,1,0:T(8,128)(2,1)}), bf16[16,64,512]{2,1,0:T(8,128)(2,1)S(1)}, u32[]{:S(2)}, u32[]{:S(2)}) async-start(bf16[16,64,512]{2,1,0:T(8,128)(2,1)} %pick_rows.1), calls=%async_computation | async-start | bytes 2097152 | tf_op jit(solution)/shard_map/all_to_all | solution.py:336
  86.2 3.5 %copy-start.11 = (s32[1024,2]{0,1:T(2,128)S(1)}, s32[1024,2]{0,1:T(2,128)}, u32[]{:S(2)}) copy-start(s32[1024,2]{0,1:T(2,128)} %param.15) | copy-start | bytes 24580
  86.2 163.8 %reduce-scatter.2.cloned.1.call-start = ((), (), s32[]{:S(2)}) async-start(), calls=%async_computation.3 | async-start | bytes 4718592 | tf_op jit(solution)/shard_map/reduce_scatter | solution.py:358
  100.8 1.2 copy-start.9
  102.8 29.0 %collective-permute-start.14 = (bf16[1472,256]{1,0:T(8,128)(2,1)}, bf16[1472,256]{1,0:T(8,128)(2,1)S(1)}, u32[]{:S(2)}, u32[]{:S(2)}) collective-permute-start(bf16[1472,256]{1,0:T(8,128)(2,1)} %slice.92), channel_id=1, source_target_pairs={{0,32},{8,40},{16,48},{24,56},{32,64},{40,72},{48,80},{56,88},{64,... | collective-permute-start | bytes 2261000 | tf_op jit(solution)/shard_map/ppermute | solution.py:33
  112.6 20.6 %collective-permute-start.15 = (bf16[1472,256]{1,0:T(8,128)(2,1)}, bf16[1472,256]{1,0:T(8,128)(2,1)S(1)}, u32[]{:S(2)}, u32[]{:S(2)}) collective-permute-start(bf16[1472,256]{1,0:T(8,128)(2,1)} %slice.93), channel_id=1, source_target_pairs={{0,96},{8,104},{16,112},{24,120},{32,0},{40,8},{48,16},{56,24},{64... | collective-permute-start | bytes 2261000 | tf_op jit(solution)/shard_map/ppermute | solution.py:33
  116.5 8.2 %copy-start.14 = (s32[4]{0:T(128)S(1)}, s32[4]{0:T(128)}, u32[]{:S(2)}) copy-start(s32[4]{0:T(128)} %param.16) | copy-start | bytes 52
  116.5 8.3 %copy-start.17 = (s32[64]{0:T(128)S(1)}, s32[64]{0:T(128)}, u32[]{:S(2)}) copy-start(s32[64]{0:T(128)} %param.20) | copy-start | bytes 772
  116.5 8.3 %copy-start.18 = (s32[4]{0:T(128)S(1)}, s32[4]{0:T(128)}, u32[]{:S(2)}) copy-start(s32[4]{0:T(128)} %param.19) | copy-start | bytes 52
  116.5 8.4 %copy-start.15 = (s32[4]{0:T(128)S(1)}, s32[4]{0:T(128)}, u32[]{:S(2)}) copy-start(s32[4]{0:T(128)} %param.17) | copy-start | bytes 52
  116.5 19.6 %collective-permute-start.6 = (bf16[1472,256]{1,0:T(8,128)(2,1)}, bf16[1472,256]{1,0:T(8,128)(2,1)}, u32[]{:S(2)}, u32[]{:S(2)}) collective-permute-start(bf16[1472,256]{1,0:T(8,128)(2,1)} %slice.85), channel_id=1, source_target_pairs={{0,8},{8,16},{16,24},{24,0},{32,40},{40,48},{48,56},{56,32},{64,72... | collective-permute-start | bytes 2261000 | tf_op jit(solution)/shard_map/ppermute | solution.py:33
  118.6 17.4 %collective-permute-start.7 = (bf16[1472,256]{1,0:T(8,128)(2,1)}, bf16[1472,256]{1,0:T(8,128)(2,1)}, u32[]{:S(2)}, u32[]{:S(2)}) collective-permute-start(bf16[1472,256]{1,0:T(8,128)(2,1)} %slice.86), channel_id=1, source_target_pairs={{0,24},{8,0},{16,8},{24,16},{32,56},{40,32},{48,40},{56,48},{64,88... | collective-permute-start | bytes 2261000 | tf_op jit(solution)/shard_map/ppermute | solution.py:33
  127.6 25.2 %copy-start.8 = (s32[13]{0:T(128)S(1)}, s32[13]{0:T(128)}, u32[]{:S(2)}) copy-start(s32[13]{0:T(128)} %pad_add_fusion.info_ref) | copy-start | bytes 160
  131.9 4.2 %copy-start.3 = (bf16[1472,256]{1,0:T(8,128)(2,1)}, bf16[1472,256]{1,0:T(8,128)(2,1)S(1)}, u32[]{:S(2)}) copy-start(bf16[1472,256]{1,0:T(8,128)(2,1)S(1)} %collective-permute-done.14.refs_8_) | copy-start | bytes 2260996
  133.2 2.9 %copy-start.5 = (bf16[1472,256]{1,0:T(8,128)(2,1)}, bf16[1472,256]{1,0:T(8,128)(2,1)S(1)}, u32[]{:S(2)}) copy-start(bf16[1472,256]{1,0:T(8,128)(2,1)S(1)} %collective-permute-done.15.refs_9_) | copy-start | bytes 2260996
  152.8 1.1 copy-start.4
  153.9 1.1 copy-start.6
  155.0 35.1 %copy-start.7 = (f32[1024,8]{1,0:T(8,128)S(1)}, f32[1024,8]{1,0:T(8,128)}, u32[]{:S(2)}) copy-start(f32[1024,8]{1,0:T(8,128)} %broadcast_multiply_fusion.gates_ref) | copy-start | bytes 98308
  190.1 2.2 copy-start.1
  209.5 2.0 copy-start.2
Sparse Core Ops, SparseCore 0:
  9.5 118.0 all-gather.2
  211.6 38.3 reduce-scatter.1

commit v2 on v1

v2 whole, which is shorter than its diff:
```python
import jax
import jax.numpy as jnp
from jax import lax
from jax.experimental import pallas as pl
from jax.experimental.pallas import tpu as pltpu
from jax.sharding import PartitionSpec as P

HD = 128
NE = 8
TOPK = 2
SIDE = 4
BF = jnp.bfloat16
F32 = jnp.float32
NEG = -1e30
adapter_scale = 0.5

ROW_Q, ROW_KV, ROW_UP, ROW_DN = 0, 512, 640, 704
SHARD_ROWS = 736
OUT_ROWS = 512
PLACES = []
for _piece, _off in ((0, 0), (1, -1), (2, 1)):
    for _i, _near in enumerate((0, -1, 1, 2)):
        PLACES.append((_piece, _i, _near, _off))
PLACES += [(3, 0, 0, 2), (3, 1, -1, 2), (4, 0, 1, 2), (4, 1, 2, 2)]


def torus(dx, dz):
    return [
        (i, ((i // SIDE + dx) % SIDE) * SIDE + (i % SIDE + dz) % SIDE) for i in range(SIDE * SIDE)
    ]


def send(value, along, step):
    return lax.ppermute(value, "req", torus(step, 0) if along == 0 else torus(0, step))


def ring(value, along):
    before = send(value, along, 1)
    after = send(value, along, -1)
    half = value.shape[0] // 2
    far_low = send(before[:half], along, 1)
    far_high = send(after[half:], along, -1)
    return before, after, far_low, far_high


def source(group, half, first, second):
    x, z = group // SIDE, group % SIDE
    dx, dz = (first, second) if half == 0 else (second, first)
    return ((x + dx + SIDE) % SIDE) * SIDE + (z + dz + SIDE) % SIDE


def pick_rows_kernel(index_ref, store_ref, out_ref):
    def one(i, carry):
        out_ref[i] = store_ref[index_ref[i]]
        return carry

    lax.fori_loop(0, out_ref.shape[0], one, 0)


def pick_rows(index, store):
    whole = pl.BlockSpec(memory_space=pltpu.VMEM)
    return pl.pallas_call(
        pick_rows_kernel,
        out_shape=jax.ShapeDtypeStruct((index.shape[0],) + store.shape[1:], store.dtype),
        in_specs=[pl.BlockSpec(memory_space=pltpu.SMEM), whole],
        out_specs=whole,
        name="pick_rows",
    )(index, store)


def pick_down_kernel(info_ref, *refs):
    pieces, (out_ref, sem) = refs[:10], refs[10:]
    group = info_ref[0]
    for j in range(4):
        slot = info_ref[1 + j]
        owner, inner = slot // 4, slot % 4
        for half in range(2):
            for piece, shard, first, second in PLACES:
                here = (owner == source(group, half, first, second)) & (inner // 2 == half)

                @pl.when(here)
                def _(piece=piece, shard=shard, half=half, j=j, inner=inner):
                    start = pl.multiple_of(shard * SHARD_ROWS + ROW_DN + (inner % 2) * 16, 16)
                    pltpu.make_async_copy(
                        pieces[half * 5 + piece].at[pl.ds(start, 16), :], out_ref.at[j], sem.at[j]
                    ).start()

    for j in range(4):
        pltpu.make_async_copy(
            pieces[0].at[pl.ds(0, 16), :], out_ref.at[j], sem.at[j]
        ).wait()


def pick_down(info, pieces):
    return pl.pallas_call(
        pick_down_kernel,
        out_shape=jax.ShapeDtypeStruct((4, 16, 256), BF),
        grid_spec=pltpu.PrefetchScalarGridSpec(
            num_scalar_prefetch=1,
            grid=(1,),
            in_specs=[pl.BlockSpec(memory_space=pltpu.HBM)] * 10,
            out_specs=pl.BlockSpec(memory_space=pl.ANY),
            scratch_shapes=[pltpu.SemaphoreType.DMA((4,))],
        ),
        name="pick_down",
    )(info, *pieces)


def start_fetch(group, pieces, row, count, target, sem):
    for half in range(2):
        for piece, shard, first, second in PLACES:
            where = pl.multiple_of(source(group, half, first, second) * count, count)
            pltpu.make_async_copy(
                pieces[half * 5 + piece].at[pl.ds(shard * SHARD_ROWS + row, count), :],
                target(half).at[pl.ds(where, count), :],
                sem(half),
            ).start()


def query_kernel(info_ref, x_ref, routes_ref, *refs):
    pieces = refs[:10]
    out_ref, wq, q, sem_q = refs[10:]
    group = info_ref[0]
    for i in range(4):
        start_fetch(
            group,
            pieces,
            ROW_Q + i * 128,
            128,
            lambda half, i=i: wq.at[half * 4 + i],
            lambda half, i=i: sem_q.at[half * 4 + i],
        )
    q[...] = jnp.zeros_like(q)

    def project(step, carry):
        e = (step % 2) * 4 + step // 2
        pltpu.make_async_copy(wq.at[e], wq.at[e], sem_q.at[e]).wait()
        for j in range(4):
            rows = pl.ds(j * 256, 256)
            value = jnp.dot(x_ref[rows, :], wq[e], preferred_element_type=F32)
            for k in range(TOPK):
                mine = routes_ref[rows, k : k + 1] == e
                q[k, rows, :] = jnp.where(mine, value, q[k, rows, :])
        return carry

    lax.fori_loop(0, NE, project, 0)
    out_ref[...] = q[...].astype(BF)


HBM = pl.BlockSpec(memory_space=pltpu.HBM)
WHOLE = pl.BlockSpec(memory_space=pltpu.VMEM)
SCALARS = pl.BlockSpec(memory_space=pltpu.SMEM)


def project_query(info, x, routes, pieces):
    return pl.pallas_call(
        query_kernel,
        out_shape=jax.ShapeDtypeStruct((TOPK, 1024, 256), BF),
        in_specs=[SCALARS, WHOLE, WHOLE] + [HBM] * 10,
        out_specs=WHOLE,
        scratch_shapes=[
            pltpu.VMEM((NE, 2048, 256), BF),
            pltpu.VMEM((TOPK, 1024, 256), F32),
            pltpu.SemaphoreType.DMA((NE,)),
        ],
        compiler_params=pltpu.CompilerParams(vmem_limit_bytes=24 * 2**20),
        name="project_query",
    )(info, x, routes, *pieces)


def attend_kernel(info_ref, x_ref, routes_ref, down_ref, q_ref, recv_ref, *refs):
    pieces = refs[:10]
    out_ref, wkv, up, cache, kv, sem_kv, sem_up, sem_cache = refs[10:]
    group = info_ref[0]
    start_fetch(
        group, pieces, ROW_UP, 64, lambda half: up.at[half], lambda half: sem_up.at[half]
    )
    start_fetch(
        group, pieces, ROW_KV, 128, lambda half: wkv.at[half], lambda half: sem_kv.at[half]
    )
    for j in range(4):
        pltpu.make_async_copy(recv_ref.at[info_ref[5 + j]], cache.at[j], sem_cache.at[j]).start()
    for half in range(2):
        pltpu.make_async_copy(up.at[half], up.at[half], sem_up.at[half]).wait()
        pltpu.make_async_copy(wkv.at[half], wkv.at[half], sem_kv.at[half]).wait()

    def project_kv(j, carry):
        rows = pl.ds(pl.multiple_of(j * 256, 256), 256)
        x = x_ref[rows, :]
        slot = info_ref[1 + j]
        down = jnp.concatenate([down_ref[e, j] for e in range(NE)], axis=1)
        low = lax.dot_general(
            x, down, (((1,), (1,)), ((), ())), preferred_element_type=F32
        ).astype(BF)
        for half in range(2):
            base = jnp.dot(x, wkv[half], preferred_element_type=F32)
            lift = up[half, pl.ds(pl.multiple_of(slot * 16, 16), 16), :]
            extra = jnp.dot(low, lift, preferred_element_type=F32)
            kv[half, rows, :] = (base + adapter_scale * extra).astype(BF)
        return carry

    lax.fori_loop(0, 4, project_kv, 0)

    for j in range(4):
        pltpu.make_async_copy(recv_ref.at[0], cache.at[j], sem_cache.at[j]).wait()

    def attend(j, carry):
        rows = pl.ds(pl.multiple_of(j * 256, 256), 256)
        cached_length = info_ref[9 + j]
        place = lax.broadcasted_iota(jnp.int32, (512, 320), 1)
        query_at = lax.broadcasted_iota(jnp.int32, (512, 320), 0) % 256
        allowed = ((place < 64) & (place < cached_length)) | (
            (place >= 64) & (place - 64 <= query_at)
        )
        for h in range(2):
            cols = slice(h * HD, (h + 1) * HD)
            keys = jnp.concatenate(
                [cache[j, :, h * 256 : h * 256 + HD], kv[h, rows, 0:HD]], axis=0
            )
            values = jnp.concatenate(
                [cache[j, :, h * 256 + HD : h * 256 + 2 * HD], kv[h, rows, HD : 2 * HD]], axis=0
            )
            queries = jnp.concatenate([q_ref[0, rows, cols], q_ref[1, rows, cols]], axis=0)
            scores = lax.dot_general(
                queries, keys, (((1,), (1,)), ((), ())), preferred_element_type=F32
            ) * (HD**-0.5)
            scores = jnp.where(allowed, scores, NEG)
            weights = jnp.exp(scores - jnp.max(scores, axis=-1, keepdims=True))
            total = jnp.sum(weights, axis=-1, keepdims=True)
            probability = (weights * (1.0 / total)).astype(BF)
            attended = jnp.dot(probability, values, preferred_element_type=F32)
            first, second = attended[:256], attended[256:]
            for e in range(NE):
                chosen = jnp.where(
                    routes_ref[rows, 0:1] == e,
                    first,
                    jnp.where(routes_ref[rows, 1:2] == e, second, 0.0),
                )
                out_ref[e, rows, cols] = chosen.astype(BF)
        return carry

    lax.fori_loop(0, 4, attend, 0)


def attention(info, x, routes, down, q, recv, pieces):
    return pl.pallas_call(
        attend_kernel,
        out_shape=jax.ShapeDtypeStruct((NE, 1024, 256), BF),
        in_specs=[SCALARS] + [WHOLE] * 4 + [HBM] * 11,
        out_specs=WHOLE,
        scratch_shapes=[
            pltpu.VMEM((2, 2048, 256), BF),
            pltpu.VMEM((2, 1024, 256), BF),
            pltpu.VMEM((4, 64, 512), BF),
            pltpu.VMEM((2, 1024, 256), BF),
            pltpu.SemaphoreType.DMA((2,)),
            pltpu.SemaphoreType.DMA((2,)),
            pltpu.SemaphoreType.DMA((4,)),
        ],
        compiler_params=pltpu.CompilerParams(vmem_limit_bytes=24 * 2**20),
        name="attention",
    )(info, x, routes, down, q, recv, *pieces)


def project_out_kernel(place_ref, gates_ref, lhs_ref, *refs):
    pieces = refs[:10]
    out_ref, w, wide, sem = refs[10:]
    group, first_block, side = place_ref[0], place_ref[1], place_ref[2]
    for half in range(2):
        for piece, shard, first, second in PLACES:
            owner = source(group, half, first, second)

            @pl.when((owner % 4) // 2 == side)
            def _(half=half, piece=piece, shard=shard, owner=owner):
                pltpu.make_async_copy(
                    pieces[half * 5 + piece].at[pl.ds(shard * OUT_ROWS, OUT_ROWS), :],
                    w.at[owner // 4, half, owner % 2],
                    sem.at[owner // 4],
                ).start()

    for e in range(NE):
        wide[e] = jnp.broadcast_to(gates_ref[:, e : e + 1], (1024, 128))

    def block(step, carry):
        at = (first_block + step) % 4
        pltpu.make_async_copy(w.at[at], w.at[at], sem.at[at]).wait()
        for i in range(4):
            rows = pl.ds(i * 256, 256)
            total = None
            for e in range(NE):
                half, pair, lane = e // 4, (e % 4) // 2, e % 2
                place = (pl.ds(pair * 256, 256), pl.ds(lane * 128, 128))
                weight = jnp.concatenate(
                    [w[at, half, 0, place[0], place[1]], w[at, half, 1, place[0], place[1]]], axis=1
                )
                value = jnp.dot(lhs_ref[e, rows, :], weight, preferred_element_type=F32)
                gate = wide[e, rows, :]
                value = value * jnp.concatenate([gate, gate], axis=1)
                total = value if total is None else total + value
            out_ref[step, rows, :] = total.astype(BF)
        return carry

    lax.fori_loop(0, 4, block, 0)


def project_out(place, gates, lhs, pieces):
    return pl.pallas_call(
        project_out_kernel,
        out_shape=jax.ShapeDtypeStruct((4, 1024, 256), BF),
        in_specs=[SCALARS, WHOLE, WHOLE] + [HBM] * 10,
        out_specs=WHOLE,
        scratch_shapes=[
            pltpu.VMEM((4, 2, 2, OUT_ROWS, 256), BF),
            pltpu.VMEM((NE, 1024, 128), F32),
            pltpu.SemaphoreType.DMA((4,)),
        ],
        compiler_params=pltpu.CompilerParams(vmem_limit_bytes=24 * 2**20),
        name="project_out",
    )(place, gates, lhs, *pieces)


def exchange(value, step):
    if step == 0:
        return lax.ppermute(value, "exp", [(i, i ^ 1) for i in range(8)])
    return lax.ppermute(value, "exp", [(i, (i + 2 * step) % 8) for i in range(8)])


def rounded_sum(*values):
    total = values[0].astype(F32)
    for value in values[1:]:
        total = total + value.astype(F32)
    return total.astype(BF)


def body(
    tokens,
    routes,
    lengths,
    cached_prefix_length,
    prefix_cache_row,
    adapter_per_request,
    adapter_storage_slot,
    router_weight,
    key_value_weight,
    expert_query_weight,
    expert_output_weight,
    adapter_down_maps,
    adapter_up_maps,
    prefix_cache_store,
):
    group = lax.axis_index("req")
    part = lax.axis_index("exp")
    query_rows = expert_query_weight.transpose(1, 0, 2).reshape(NE * 128, 256)
    down_rows = (
        lax.dynamic_slice_in_dim(adapter_down_maps, part * 256, 256, 1)
        .transpose(0, 2, 1)
        .reshape(64, 256)
    )
    up_rows = adapter_up_maps.reshape(64, 512)
    out_rows = (
        expert_output_weight.reshape(4, 2, 256, 128).transpose(0, 2, 1, 3).reshape(1024, 256)
    )
    near_mix, near_out = [], []
    for half in range(2):
        cols = slice(half * 256, half * 256 + 256)
        own = jnp.concatenate(
            [
                query_rows[half * 512 : half * 512 + 512],
                key_value_weight[:, cols],
                up_rows[:, cols],
                down_rows[half * 32 : half * 32 + 32],
                out_rows[half * 512 : half * 512 + 512],
            ],
            axis=0,
        )
        before, after, far_low, far_high = ring(own, half)
        cut = SHARD_ROWS - far_low.shape[0]
        near_mix.append(
            jnp.concatenate(
                [own[:SHARD_ROWS], before[:SHARD_ROWS], after[:SHARD_ROWS], far_low, far_high[:cut]],
                axis=0,
            )
        )
        near_out.append(
            jnp.concatenate(
                [own[SHARD_ROWS:], before[SHARD_ROWS:], after[SHARD_ROWS:], far_high[cut:]], axis=0
            )
        )
    pieces, waits = [], []
    for half in range(2):
        rest = ring(near_mix[half], 1 - half)
        pieces += [near_mix[half], *rest]
        waits += rest[:2]
    near_out = lax.optimization_barrier(tuple(near_out + waits))[:2]
    out_pieces = []
    for half in range(2):
        out_pieces += [near_out[half], *ring(near_out[half], 1 - half)]

    rows_by_group = prefix_cache_row.reshape(16, 4)
    held = (rows_by_group == group).astype(jnp.int32)
    wanted_by = jnp.sum(held * jnp.arange(4, dtype=jnp.int32)[None, :], axis=1)
    outgoing = pick_rows(wanted_by, prefix_cache_store)
    received = lax.all_to_all(outgoing, "req", split_axis=0, concat_axis=0, tiled=True)

    adapter_hot = (
        adapter_per_request[:, None]
        == jnp.arange(adapter_storage_slot.shape[0], dtype=jnp.int32)[None, :]
    ).astype(jnp.int32)
    slots = jnp.sum(adapter_hot * adapter_storage_slot[None, :], axis=1)
    own_rows = lax.dynamic_slice_in_dim(prefix_cache_row, group * 4, 4, 0)
    info = jnp.concatenate([group[None].astype(jnp.int32), slots, own_rows, cached_prefix_length])

    logits = jnp.dot(tokens, router_weight, preferred_element_type=F32)
    expert = jnp.arange(NE, dtype=jnp.int32)
    route_hot = (routes[:, :, None] == expert[None, None, :]).astype(F32)
    chosen = jnp.sum(route_hot * logits[:, None, :], axis=-1)
    gate_values = jax.nn.sigmoid(chosen - chosen[:, ::-1])
    live = (jnp.arange(256, dtype=jnp.int32)[None, :] < lengths[:, None]).reshape(1024, 1)
    gates = jnp.sum(route_hot * gate_values[:, :, None], axis=1) * live.astype(F32)

    down_part = pick_down(info, pieces)
    down = lax.all_to_all(
        jnp.broadcast_to(down_part[None], (NE, 4, 16, 256)), "exp", 0, 0, tiled=True
    )
    q = project_query(info, tokens, routes, pieces)
    lhs = attention(info, tokens, routes, down, q, received, pieces)

    y, core = part // 2, part % 2
    theirs_at = jnp.stack([group, y, 1 - core]).astype(jnp.int32)
    mine_at = jnp.stack([group, y, core]).astype(jnp.int32)
    theirs = project_out(theirs_at, gates, lhs, out_pieces)
    swapped = exchange(theirs, 0)
    mine = project_out(mine_at, gates, lhs, out_pieces)
    both = rounded_sum(mine, swapped)
    low = exchange(both[2, :512], 1)
    high = exchange(both[2, 512:], -1)
    ahead = jnp.concatenate([rounded_sum(both[1, :512], low), both[1, 512:]], axis=0)
    behind = jnp.concatenate([both[3, :512], rounded_sum(both[3, 512:], high)], axis=0)
    return rounded_sum(both[0], exchange(ahead, 1), exchange(behind, -1))


def solution(mesh):
    return jax.shard_map(
        body,
        mesh=mesh,
        in_specs=(
            P("req", None),
            P("req", None),
            P("req"),
            P("req"),
            P(),
            P("req"),
            P(),
            P(),
            P("req", "exp"),
            P("req", None, "exp"),
            P(None, "exp", "req"),
            P("req", None, None),
            P("req", None, "exp"),
            P("req", None, "exp"),
        ),
        out_specs=P("req", "exp"),
        check_vma=False,
    )
```

time: 258 us -> 256 us (level)
  Pallas kernels: 88.9 us -> 65 us
  starting transfers between devices: 31.4 us -> 52.6 us
  local copies, waits for them, and re-layouts: 27 us -> 43.2 us
  blocking collectives: 13.8 us -> 0 us
  between operations: 13.7 us -> 0.72 us
  waiting for transfers between devices: 74.9 us -> 82.1 us
  other arithmetic: 3.65 us -> 7.61 us
    reduce_scatter x1 -> x0, waiting for transfers between devices: 38.5 us -> none  [body(): lax.psum_scatter(partial_value, 'exp', scatter_dimension=1, tiled=True)]
    ppermute x16 -> x24, waiting for transfers between devices: 35.6 us -> 61 us  [send(): lax.ppermute(value, 'req', torus(step, 0) if along == 0 else torus(0, step))]
    pallas_call x3 -> x5, Pallas kernels: 86.1 us -> 62 us  [the longest x1 21.3 us: attention(): pl.pallas_call(attend_kernel, out_shape=jax.ShapeDtypeStruct((NE, 1024, 2...]
    ppermute x0 -> x5, waiting for transfers between devices: none -> 21.1 us  [the longest x4 21.1 us: exchange(): lax.ppermute(value, 'exp', [(i, (i + 2 * step) % 8) for i in range(8)])]
    all_gather x1 -> x0, blocking collectives: 13.8 us -> none  [body(): lax.all_gather(down_part.reshape(1, 4, 16, 256), 'exp', axis=0, tiled=True)]
    ppermute x16 -> x24, starting transfers between devices: 24.6 us -> 36.5 us  [send(): lax.ppermute(value, 'req', torus(step, 0) if along == 0 else torus(0, step))]
    unnamed x49 -> x103, local copies, waits for them, and re-layouts: 14.3 us -> 24.1 us
    ppermute x0 -> x5, starting transfers between devices: none -> 6.24 us  [the longest x4 5.55 us: exchange(): lax.ppermute(value, 'exp', [(i, (i + 2 * step) % 8) for i in range(8)])]
  transfers between devices with their start and end apart: 19 -> 31, of which waited for: 11 -> 11; matrix products, arithmetic and copies ran while one was open for 10% -> 10% of each run, Pallas kernels for 28% -> 22%
where the time goes in v2:
time: 256 us; the launch traced here: 252 us
  waiting for transfers between devices  82.1 us (32%)
  Pallas kernels  65 us (25%)
  starting transfers between devices  52.6 us (21%)
  local copies, waits for them, and re-layouts  43.2 us (17%)
  other arithmetic  7.61 us (3%)
    ppermute x24, waiting for transfers between devices, send(): lax.ppermute(value, 'req', torus(step, 0) if along == 0 else torus(0, step))  61 us
    ppermute x24, starting transfers between devices, send(): lax.ppermute(value, 'req', torus(step, 0) if along == 0 else torus(0, step))  36.5 us
    unnamed x103, local copies, waits for them, and re-layouts  24.1 us
    pallas_call x1, Pallas kernels, attention(): pl.pallas_call(attend_kernel, out_shape=jax.ShapeDtypeStruct((NE, 1024, 2...  21.3 us
    ppermute x4, waiting for transfers between devices, exchange(): lax.ppermute(value, 'exp', [(i, (i + 2 * step) % 8) for i in range(8)])  21.1 us
    pallas_call x1, Pallas kernels, project_query(): pl.pallas_call(query_kernel, out_shape=jax.ShapeDtypeStruct((TOPK, 1024,...  20.3 us
    pallas_call x2, Pallas kernels, project_out(): pl.pallas_call(project_out_kernel, out_shape=jax.ShapeDtypeStruct((4, 102...  18.3 us
    slice x6, local copies, waits for them, and re-layouts, ring(): far_high = send(after[half:], along, -1)  6.86 us
  transfers between devices with their start and end apart: 31, of which 11 were waited for; matrix products, arithmetic and copies ran while one was open for 10% of the time, Pallas kernels for 22%

profile of v2, /device:TPU:6, one launch (start us, length us, event | category | flops | bytes accessed | tf_op | source)
XLA Modules:
  0.0 252.5 jit_solution(17923701059359375073)
XLA Ops:
  0.0 0.9 copy-done
  1.0 1.6 copy.45
  4.1 4.1 %collective-permute-start.9 = (bf16[1248,256]{1,0:T(8,128)(2,1)S(1)}, bf16[1248,256]{1,0:T(8,128)(2,1)S(1)}, u32[]{:S(2)}, u32[]{:S(2)}) collective-permute-start(bf16[1248,256]{1,0:T(8,128)(2,1)S(1)} %constant_dynamic-update-slice_fusion.8), channel_id=1, source_target_pairs={{0,24},{8,0},{16,8},{24,16},{32,56},{40,32},{48,40},{56,48},{64,88... | collective-permute-start | bytes 1916936 | tf_op jit(solution)/shard_map/ppermute | solution.py:34
  9.2 2.4 collective-permute-start
  11.6 10.3 %collective-permute-done.9 = bf16[1248,256]{1,0:T(8,128)(2,1)S(1)} collective-permute-done((bf16[1248,256]{1,0:T(8,128)(2,1)S(1)}, bf16[1248,256]{1,0:T(8,128)(2,1)S(1)}, u32[]{:S(2)}, u32[]{:S(2)}) %collective-permute-start.9) | collective-permute-done | bytes 639008 | tf_op jit(solution)/shard_map/ppermute | solution.py:34
  21.9 3.8 %collective-permute-start.11 = (bf16[624,256]{1,0:T(8,128)(2,1)S(1)}, bf16[624,256]{1,0:T(8,128)(2,1)S(1)}, u32[]{:S(2)}, u32[]{:S(2)}) collective-permute-start(bf16[624,256]{1,0:T(8,128)(2,1)S(1)} %slice.210), channel_id=1, source_target_pairs={{0,24},{8,0},{16,8},{24,16},{32,56},{40,32},{48,40},{56,48},{64,88... | collective-permute-start | bytes 958472 | tf_op jit(solution)/shard_map/ppermute | solution.py:34
  26.8 2.5 collective-permute-start.2
  29.4 5.7 %collective-permute-done.10 = bf16[624,256]{1,0:T(8,128)(2,1)S(1)} collective-permute-done((bf16[624,256]{1,0:T(8,128)(2,1)S(1)}, bf16[624,256]{1,0:T(8,128)(2,1)S(1)}, u32[]{:S(2)}, u32[]{:S(2)}) %collective-permute-start.10) | collective-permute-done | bytes 319520 | tf_op jit(solution)/shard_map/ppermute | solution.py:34
  36.1 2.4 collective-permute-start.12
  39.1 1.5 collective-permute-start.4
  41.8 1.0 pad_maximum_fusion.1.refs_5_
  42.8 1.0 pad_maximum_fusion.refs_0_
  43.9 25.2 %collective-permute-done.13.refs_7_ = bf16[2944,256]{1,0:T(8,128)(2,1)S(1)} collective-permute-done((bf16[2944,256]{1,0:T(8,128)(2,1)S(1)}, bf16[2944,256]{1,0:T(8,128)(2,1)S(1)}, u32[]{:S(2)}, u32[]{:S(2)}) %collective-permute-start.13) | collective-permute-done | bytes 1507360 | tf_op jit(solution)/shard_map/ppermute | solution.py:34
  69.1 1.7 collective-permute-done.5.refs_2_
  70.8 1.3 collective-permute-done.4.refs_1_
  72.4 1.7 collective-permute-start.16
  74.3 3.3 %collective-permute-start.20 = (bf16[2048,256]{1,0:T(8,128)(2,1)}, bf16[2048,256]{1,0:T(8,128)(2,1)}, u32[]{:S(2)}, u32[]{:S(2)}) collective-permute-start(bf16[2048,256]{1,0:T(8,128)(2,1)} %pad_maximum_fusion.1.refs_5_), channel_id=1, source_target_pairs={{0,32},{8,40},{16,48},{24,56},{32,64},{40,72},{48,80},{56,88},{64,... | collective-permute-start | bytes 3145736 | tf_op jit(solution)/shard_map/ppermute | solution.py:34
  78.2 2.1 pick_rows.1
  80.3 5.5 %all-to-all-start.1 = ((bf16[16,64,512]{2,1,0:T(8,128)(2,1)}), bf16[16,64,512]{2,1,0:T(8,128)(2,1)}, u32[]{:S(2)}, u32[]{:S(2)}) async-start(bf16[16,64,512]{2,1,0:T(8,128)(2,1)} %pick_rows.1), calls=%async_computation.1 | async-start | bytes 2097152 | tf_op jit(solution)/shard_map/all_to_all | solution.py:403
  88.5 2.0 slice.202
  90.6 11.1 %collective-permute-done.17.refs_2_ = bf16[2048,256]{1,0:T(8,128)(2,1)} collective-permute-done((bf16[2048,256]{1,0:T(8,128)(2,1)}, bf16[2048,256]{1,0:T(8,128)(2,1)}, u32[]{:S(2)}, u32[]{:S(2)}) %collective-permute-start.17) | collective-permute-done | bytes 1048608 | tf_op jit(solution)/shard_map/ppermute | solution.py:34
  101.7 3.5 %collective-permute-start.7 = (bf16[1472,256]{1,0:T(8,128)(2,1)}, bf16[1472,256]{1,0:T(8,128)(2,1)S(1)}, u32[]{:S(2)}, u32[]{:S(2)}) collective-permute-start(bf16[1472,256]{1,0:T(8,128)(2,1)} %slice.202), channel_id=1, source_target_pairs={{0,24},{8,0},{16,8},{24,16},{32,56},{40,32},{48,40},{56,48},{64,88... | collective-permute-start | bytes 2261000 | tf_op jit(solution)/shard_map/ppermute | solution.py:34
  105.2 1.2 fusion.7
  106.6 1.2 slice.201
  108.1 1.9 slice.221
  109.9 1.9 slice.220
  111.8 2.0 slice.223
  113.8 3.2 %collective-permute-start.19 = (bf16[1024,256]{1,0:T(8,128)(2,1)}, bf16[1024,256]{1,0:T(8,128)(2,1)}, u32[]{:S(2)}, u32[]{:S(2)}) collective-permute-start(bf16[1024,256]{1,0:T(8,128)(2,1)} %slice.221), channel_id=1, source_target_pairs={{0,24},{8,0},{16,8},{24,16},{32,56},{40,32},{48,40},{56,48},{64,88... | collective-permute-start | bytes 1572872 | tf_op jit(solution)/shard_map/ppermute | solution.py:34
  117.0 1.9 slice.222
  118.9 5.6 %collective-permute-done.15.refs_9_ = bf16[1472,256]{1,0:T(8,128)(2,1)S(1)} collective-permute-done((bf16[1472,256]{1,0:T(8,128)(2,1)}, bf16[1472,256]{1,0:T(8,128)(2,1)S(1)}, u32[]{:S(2)}, u32[]{:S(2)}) %collective-permute-start.15) | collective-permute-done | bytes 753696 | tf_op jit(solution)/shard_map/ppermute | solution.py:34
  124.8 3.2 %collective-permute-start.22 = (bf16[1024,256]{1,0:T(8,128)(2,1)}, bf16[1024,256]{1,0:T(8,128)(2,1)}, u32[]{:S(2)}, u32[]{:S(2)}) collective-permute-start(bf16[1024,256]{1,0:T(8,128)(2,1)} %slice.222), channel_id=1, source_target_pairs={{0,32},{8,40},{16,48},{24,56},{32,64},{40,72},{48,80},{56,88},{64,... | collective-permute-start | bytes 1572872 | tf_op jit(solution)/shard_map/ppermute | solution.py:34
  128.0 1.0 copy.34.routes_ref
  129.2 1.0 copy.29
  131.0 3.0 %pick_down.1 = bf16[4,16,256]{2,1,0:T(8,128)(2,1)} custom-call(s32[13]{0:T(128)} %pad_add_fusion.2.info_ref, bf16[2944,256]{1,0:T(8,128)(2,1)} %copy-done.8, bf16[2944,256]{1,0:T(8,128)(2,1)} %collective-permute-done.4.refs_1_, bf16[2944,256]{1,0:T(8,128)(2,1)} %collective-permute-done.5.refs_2_, bf16[1472,256]{1,0:T(8,128)(2,1)} %collective-permute-done.6.refs_3_, ...), custom_call_target="tpu_custom_call" | custom-call | tf_op jit(solution)/shard_map/pick_down/pallas_call | solution.py:95
  134.1 1.6 broadcast_in_dim.2
  135.7 4.5 %all-to-all-start = ((bf16[8,4,16,256]{3,2,1,0:T(8,128)(2,1)}), bf16[8,4,16,256]{3,2,1,0:T(8,128)(2,1)S(1)}, u32[]{:S(2)}, u32[]{:S(2)}) async-start(bf16[8,4,16,256]{3,2,1,0:T(8,128)(2,1)} %broadcast_in_dim.2), calls=%async_computation | async-start | bytes 524288 | tf_op jit(solution)/shard_map/all_to_all | solution.py:422
  140.2 2.0 broadcast_multiply_fusion.gates_ref
  142.2 2.2 copy-done.2
  144.4 1.4 copy-done.9
  145.8 1.4 copy-done.12
  147.2 1.1 copy-done.15
  148.3 1.1 copy-done.18
  149.4 1.1 copy-done.21
  150.5 1.0 copy-done.24
  151.6 20.3 %project_query.1.q_ref = bf16[2,1024,256]{2,1,0:T(8,128)(2,1)S(1)} custom-call(s32[13]{0:T(128)S(1)} %copy-done.28, bf16[1024,2048]{1,0:T(8,128)(2,1)S(1)} %copy-done.2, s32[1024,2]{1,0:T(8,128)S(1)} %copy-done.24, bf16[2944,256]{1,0:T(8,128)(2,1)S(1)} %copy-done.9, bf16[2944,256]{1,0:T(8,128)(2,1)} %collective-permute-done.4.refs_1_, ...), custom_call_target="tpu_custom_call" | custom-call | tf_op jit(solution)/shard_map/project_query/pallas_call | solution.py:156
  171.9 1.0 copy-done.26
  172.9 2.2 copy-done.3
  175.1 1.4 copy-done.10
  176.5 1.4 copy-done.13
  177.9 1.1 copy-done.16
  179.0 1.1 copy-done.19
  180.1 1.1 copy-done.22
  181.3 1.0 copy-done.25
  182.3 1.2 copy-done.27
  183.5 21.3 %attention.1.lhs_ref = bf16[8,1024,256]{2,1,0:T(8,128)(2,1)S(1)} custom-call(s32[13]{0:T(128)S(1)} %copy-done.28, bf16[1024,2048]{1,0:T(8,128)(2,1)S(1)} %copy-done.3, s32[1024,2]{1,0:T(8,128)S(1)} %copy-done.25, bf16[8,4,16,256]{3,2,1,0:T(8,128)(2,1)S(1)} %all-to-all-done.down_ref, bf16[2,1024,256]{2,1,0:T(8,128)(2,1)S(1)} %copy-done.27, ...), custom_call_target="tpu_custom_call" | custom-call | tf_op jit(solution)/shard_map/attention/pallas_call | solution.py:246
  204.9 9.2 %project_out.3 = bf16[4,1024,256]{2,1,0:T(8,128)(2,1)S(1)} custom-call(s32[3]{0:T(128)S(1)} %pad_add_fusion.3.place_ref, f32[1024,8]{1,0:T(8,128)S(1)} %copy-done.23, bf16[8,1024,256]{2,1,0:T(8,128)(2,1)S(1)} %attention.1.lhs_ref, bf16[2048,256]{1,0:T(8,128)(2,1)} %pad_maximum_fusion.refs_0_, bf16[2048,256]{1,0:T(8,128)(2,1)} %collective-permute-done.16.refs_1_, ...), custom_call_target="tpu_custom_call" | custom-call | tf_op jit(solution)/shard_map/project_out/pallas_call | solution.py:307
  214.9 9.1 %project_out.2 = bf16[4,1024,256]{2,1,0:T(8,128)(2,1)S(1)} custom-call(s32[3]{0:T(128)S(1)} %pad_add_fusion.place_ref, f32[1024,8]{1,0:T(8,128)S(1)} %copy-done.23, bf16[8,1024,256]{2,1,0:T(8,128)(2,1)S(1)} %attention.1.lhs_ref, bf16[2048,256]{1,0:T(8,128)(2,1)} %pad_maximum_fusion.refs_0_, bf16[2048,256]{1,0:T(8,128)(2,1)} %collective-permute-done.16.refs_1_, ...), custom_call_target="tpu_custom_call" | custom-call | tf_op jit(solution)/shard_map/project_out/pallas_call | solution.py:307
  224.6 2.0 collective-permute-start.25
  226.6 1.3 collective-permute-start.27
  227.9 6.4 %collective-permute-done.25 = bf16[512,256]{1,0:T(8,128)(2,1)S(1)} collective-permute-done((bf16[512,256]{1,0:T(8,128)(2,1)S(1)}, bf16[512,256]{1,0:T(8,128)(2,1)S(1)}, u32[]{:S(2)}, u32[]{:S(2)}) %collective-permute-start.25) | collective-permute-done | bytes 262176 | tf_op jit(solution)/shard_map/ppermute | solution.py:325
  235.3 2.2 collective-permute-start.28
  237.6 11.1 %collective-permute-done.28 = bf16[1024,256]{1,0:T(8,128)(2,1)S(1)} collective-permute-done((bf16[1024,256]{1,0:T(8,128)(2,1)S(1)}, bf16[1024,256]{1,0:T(8,128)(2,1)S(1)}, u32[]{:S(2)}, u32[]{:S(2)}) %collective-permute-start.28) | collective-permute-done | bytes 524320 | tf_op jit(solution)/shard_map/ppermute | solution.py:325
  248.7 2.7 %collective-permute-done.26 = bf16[1024,256]{1,0:T(8,128)(2,1)S(1)} collective-permute-done((bf16[1024,256]{1,0:T(8,128)(2,1)S(1)}, bf16[1024,256]{1,0:T(8,128)(2,1)S(1)}, u32[]{:S(2)}, u32[]{:S(2)}) %collective-permute-start.26) | collective-permute-done | bytes 524320 | tf_op jit(solution)/shard_map/ppermute | solution.py:325
  251.5 1.0 fusion.1
  (166 shorter events, 14.2 us)
Async XLA Ops:
  0.0 2.9 %copy-start.34 = (bf16[128,8,256]{2,1,0:T(8,128)(2,1)S(1)}, bf16[128,8,256]{2,1,0:T(8,128)(2,1)}, u32[]{:S(2)}) copy-start(bf16[128,8,256]{2,1,0:T(8,128)(2,1)} %param.23) | copy-start | bytes 1572868
  4.1 17.7 %collective-permute-start.9 = (bf16[1248,256]{1,0:T(8,128)(2,1)S(1)}, bf16[1248,256]{1,0:T(8,128)(2,1)S(1)}, u32[]{:S(2)}, u32[]{:S(2)}) collective-permute-start(bf16[1248,256]{1,0:T(8,128)(2,1)S(1)} %constant_dynamic-update-slice_fusion.8), channel_id=1, source_target_pairs={{0,24},{8,0},{16,8},{24,16},{32,56},{40,32},{48,40},{56,48},{64,88... | collective-permute-start | bytes 1916936 | tf_op jit(solution)/shard_map/ppermute | solution.py:34
  8.2 17.4 %collective-permute-start.8 = (bf16[1248,256]{1,0:T(8,128)(2,1)S(1)}, bf16[1248,256]{1,0:T(8,128)(2,1)S(1)}, u32[]{:S(2)}, u32[]{:S(2)}) collective-permute-start(bf16[1248,256]{1,0:T(8,128)(2,1)S(1)} %constant_dynamic-update-slice_fusion.8), channel_id=1, source_target_pairs={{0,8},{8,16},{16,24},{24,0},{32,40},{40,48},{48,56},{56,32},{64,72... | collective-permute-start | bytes 1916936 | tf_op jit(solution)/shard_map/ppermute | solution.py:34
  8.3 17.5 %collective-permute-start.1 = (bf16[1248,256]{1,0:T(8,128)(2,1)S(1)}, bf16[1248,256]{1,0:T(8,128)(2,1)S(1)}, u32[]{:S(2)}, u32[]{:S(2)}) collective-permute-start(bf16[1248,256]{1,0:T(8,128)(2,1)S(1)} %constant_dynamic-update-slice_fusion), channel_id=1, source_target_pairs={{0,96},{8,104},{16,112},{24,120},{32,0},{40,8},{48,16},{56,24},{64... | collective-permute-start | bytes 1916936 | tf_op jit(solution)/shard_map/ppermute | solution.py:34
  9.2 17.6 %collective-permute-start = (bf16[1248,256]{1,0:T(8,128)(2,1)S(1)}, bf16[1248,256]{1,0:T(8,128)(2,1)S(1)}, u32[]{:S(2)}, u32[]{:S(2)}) collective-permute-start(bf16[1248,256]{1,0:T(8,128)(2,1)S(1)} %constant_dynamic-update-slice_fusion), channel_id=1, source_target_pairs={{0,32},{8,40},{16,48},{24,56},{32,64},{40,72},{48,80},{56,88},{64,... | collective-permute-start | bytes 1916936 | tf_op jit(solution)/shard_map/ppermute | solution.py:34
  21.9 18.8 %copy-start.29 = (bf16[1248,256]{1,0:T(8,128)(2,1)}, bf16[1248,256]{1,0:T(8,128)(2,1)S(1)}, u32[]{:S(2)}) copy-start(bf16[1248,256]{1,0:T(8,128)(2,1)S(1)} %collective-permute-done.9) | copy-start | bytes 1916932
  21.9 13.2 %collective-permute-start.11 = (bf16[624,256]{1,0:T(8,128)(2,1)S(1)}, bf16[624,256]{1,0:T(8,128)(2,1)S(1)}, u32[]{:S(2)}, u32[]{:S(2)}) collective-permute-start(bf16[624,256]{1,0:T(8,128)(2,1)S(1)} %slice.210), channel_id=1, source_target_pairs={{0,24},{8,0},{16,8},{24,16},{32,56},{40,32},{48,40},{56,48},{64,88... | collective-permute-start | bytes 958472 | tf_op jit(solution)/shard_map/ppermute | solution.py:34
  25.7 15.1 %copy-start.30 = (bf16[1248,256]{1,0:T(8,128)(2,1)}, bf16[1248,256]{1,0:T(8,128)(2,1)S(1)}, u32[]{:S(2)}) copy-start(bf16[1248,256]{1,0:T(8,128)(2,1)S(1)} %collective-permute-done.8) | copy-start | bytes 1916932
  25.7 9.4 %collective-permute-start.10 = (bf16[624,256]{1,0:T(8,128)(2,1)S(1)}, bf16[624,256]{1,0:T(8,128)(2,1)S(1)}, u32[]{:S(2)}, u32[]{:S(2)}) collective-permute-start(bf16[624,256]{1,0:T(8,128)(2,1)S(1)} %slice.209), channel_id=1, source_target_pairs={{0,8},{8,16},{16,24},{24,0},{32,40},{40,48},{48,56},{56,32},{64,72... | collective-permute-start | bytes 958472 | tf_op jit(solution)/shard_map/ppermute | solution.py:34
  25.8 15.0 %copy-start.31 = (bf16[1248,256]{1,0:T(8,128)(2,1)}, bf16[1248,256]{1,0:T(8,128)(2,1)S(1)}, u32[]{:S(2)}) copy-start(bf16[1248,256]{1,0:T(8,128)(2,1)S(1)} %collective-permute-done.1) | copy-start | bytes 1916932
  25.8 12.7 %collective-permute-start.3 = (bf16[624,256]{1,0:T(8,128)(2,1)S(1)}, bf16[624,256]{1,0:T(8,128)(2,1)S(1)}, u32[]{:S(2)}, u32[]{:S(2)}) collective-permute-start(bf16[624,256]{1,0:T(8,128)(2,1)S(1)} %slice.199), channel_id=1, source_target_pairs={{0,96},{8,104},{16,112},{24,120},{32,0},{40,8},{48,16},{56,24},{64... | collective-permute-start | bytes 958472 | tf_op jit(solution)/shard_map/ppermute | solution.py:34
  26.7 14.0 %copy-start.32 = (bf16[1248,256]{1,0:T(8,128)(2,1)}, bf16[1248,256]{1,0:T(8,128)(2,1)S(1)}, u32[]{:S(2)}) copy-start(bf16[1248,256]{1,0:T(8,128)(2,1)S(1)} %collective-permute-done) | copy-start | bytes 1916932
  26.8 11.7 %collective-permute-start.2 = (bf16[624,256]{1,0:T(8,128)(2,1)S(1)}, bf16[624,256]{1,0:T(8,128)(2,1)S(1)}, u32[]{:S(2)}, u32[]{:S(2)}) collective-permute-start(bf16[624,256]{1,0:T(8,128)(2,1)S(1)} %slice.198), channel_id=1, source_target_pairs={{0,32},{8,40},{16,48},{24,56},{32,64},{40,72},{48,80},{56,88},{64,... | collective-permute-start | bytes 958472 | tf_op jit(solution)/shard_map/ppermute | solution.py:34
  35.1 5.6 %copy-start.11 = (bf16[2944,256]{1,0:T(8,128)(2,1)}, bf16[2944,256]{1,0:T(8,128)(2,1)S(1)}, u32[]{:S(2)}) copy-start(bf16[2944,256]{1,0:T(8,128)(2,1)S(1)} %slice_dynamic-update-slice_fusion.8.refs_5_) | copy-start | bytes 4521988
  35.2 33.9 %collective-permute-start.13 = (bf16[2944,256]{1,0:T(8,128)(2,1)S(1)}, bf16[2944,256]{1,0:T(8,128)(2,1)S(1)}, u32[]{:S(2)}, u32[]{:S(2)}) collective-permute-start(bf16[2944,256]{1,0:T(8,128)(2,1)S(1)} %slice_dynamic-update-slice_fusion.8.refs_5_), channel_id=1, source_target_pairs={{0,96},{8,104},{16,112},{24,120},{32,0},{40,8},{48,16},{56,24},{64... | collective-permute-start | bytes 4521992 | tf_op jit(solution)/shard_map/ppermute | solution.py:34
  36.1 33.0 %collective-permute-start.12 = (bf16[2944,256]{1,0:T(8,128)(2,1)S(1)}, bf16[2944,256]{1,0:T(8,128)(2,1)S(1)}, u32[]{:S(2)}, u32[]{:S(2)}) collective-permute-start(bf16[2944,256]{1,0:T(8,128)(2,1)S(1)} %slice_dynamic-update-slice_fusion.8.refs_5_), channel_id=1, source_target_pairs={{0,32},{8,40},{16,48},{24,56},{32,64},{40,72},{48,80},{56,88},{64,... | collective-permute-start | bytes 4521992 | tf_op jit(solution)/shard_map/ppermute | solution.py:34
  38.5 2.3 copy-start.33
  38.5 2.3 copy-start.8
  38.5 32.3 %collective-permute-start.5 = (bf16[2944,256]{1,0:T(8,128)(2,1)S(1)}, bf16[2944,256]{1,0:T(8,128)(2,1)}, u32[]{:S(2)}, u32[]{:S(2)}) collective-permute-start(bf16[2944,256]{1,0:T(8,128)(2,1)S(1)} %slice_dynamic-update-slice_fusion.9.refs_0_), channel_id=1, source_target_pairs={{0,24},{8,0},{16,8},{24,16},{32,56},{40,32},{48,40},{56,48},{64,88... | collective-permute-start | bytes 4521992 | tf_op jit(solution)/shard_map/ppermute | solution.py:34
  39.1 33.0 %collective-permute-start.4 = (bf16[2944,256]{1,0:T(8,128)(2,1)S(1)}, bf16[2944,256]{1,0:T(8,128)(2,1)}, u32[]{:S(2)}, u32[]{:S(2)}) collective-permute-start(bf16[2944,256]{1,0:T(8,128)(2,1)S(1)} %slice_dynamic-update-slice_fusion.9.refs_0_), channel_id=1, source_target_pairs={{0,8},{8,16},{16,24},{24,0},{32,40},{40,48},{48,56},{56,32},{64,72... | collective-permute-start | bytes 4521992 | tf_op jit(solution)/shard_map/ppermute | solution.py:34
  40.8 2.0 slice-start.2
  40.8 2.0 slice-start.3
  40.9 2.0 slice-start.4
  42.8 31.4 %copy-start.41 = (s32[64]{0:T(128)S(1)}, s32[64]{0:T(128)}, u32[]{:S(2)}) copy-start(s32[64]{0:T(128)} %param.18) | copy-start | bytes 772
  69.1 16.7 %copy-start.4 = (bf16[2944,256]{1,0:T(8,128)(2,1)}, bf16[2944,256]{1,0:T(8,128)(2,1)S(1)}, u32[]{:S(2)}) copy-start(bf16[2944,256]{1,0:T(8,128)(2,1)S(1)} %collective-permute-done.13.refs_7_) | copy-start | bytes 4521988
  69.1 18.5 %copy-start.6 = (bf16[2944,256]{1,0:T(8,128)(2,1)}, bf16[2944,256]{1,0:T(8,128)(2,1)S(1)}, u32[]{:S(2)}) copy-start(bf16[2944,256]{1,0:T(8,128)(2,1)S(1)} %collective-permute-done.12.refs_6_) | copy-start | bytes 4521988
  72.1 29.5 %collective-permute-start.17 = (bf16[2048,256]{1,0:T(8,128)(2,1)}, bf16[2048,256]{1,0:T(8,128)(2,1)}, u32[]{:S(2)}, u32[]{:S(2)}) collective-permute-start(bf16[2048,256]{1,0:T(8,128)(2,1)} %pad_maximum_fusion.refs_0_), channel_id=1, source_target_pairs={{0,24},{8,0},{16,8},{24,16},{32,56},{40,32},{48,40},{56,48},{64,88... | collective-permute-start | bytes 3145736 | tf_op jit(solution)/shard_map/ppermute | solution.py:34
  72.4 29.2 %collective-permute-start.16 = (bf16[2048,256]{1,0:T(8,128)(2,1)}, bf16[2048,256]{1,0:T(8,128)(2,1)}, u32[]{:S(2)}, u32[]{:S(2)}) collective-permute-start(bf16[2048,256]{1,0:T(8,128)(2,1)} %pad_maximum_fusion.refs_0_), channel_id=1, source_target_pairs={{0,8},{8,16},{16,24},{24,0},{32,40},{40,48},{48,56},{56,32},{64,72... | collective-permute-start | bytes 3145736 | tf_op jit(solution)/shard_map/ppermute | solution.py:34
  74.2 33.6 %collective-permute-start.21 = (bf16[2048,256]{1,0:T(8,128)(2,1)}, bf16[2048,256]{1,0:T(8,128)(2,1)}, u32[]{:S(2)}, u32[]{:S(2)}) collective-permute-start(bf16[2048,256]{1,0:T(8,128)(2,1)} %pad_maximum_fusion.1.refs_5_), channel_id=1, source_target_pairs={{0,96},{8,104},{16,112},{24,120},{32,0},{40,8},{48,16},{56,24},{64... | collective-permute-start | bytes 3145736 | tf_op jit(solution)/shard_map/ppermute | solution.py:34
  74.3 39.5 %collective-permute-start.20 = (bf16[2048,256]{1,0:T(8,128)(2,1)}, bf16[2048,256]{1,0:T(8,128)(2,1)}, u32[]{:S(2)}, u32[]{:S(2)}) collective-permute-start(bf16[2048,256]{1,0:T(8,128)(2,1)} %pad_maximum_fusion.1.refs_5_), channel_id=1, source_target_pairs={{0,32},{8,40},{16,48},{24,56},{32,64},{40,72},{48,80},{56,88},{64,... | collective-permute-start | bytes 3145736 | tf_op jit(solution)/shard_map/ppermute | solution.py:34
  80.3 53.7 %all-to-all-start.1 = ((bf16[16,64,512]{2,1,0:T(8,128)(2,1)}), bf16[16,64,512]{2,1,0:T(8,128)(2,1)}, u32[]{:S(2)}, u32[]{:S(2)}) async-start(bf16[16,64,512]{2,1,0:T(8,128)(2,1)} %pick_rows.1), calls=%async_computation.1 | async-start | bytes 2097152 | tf_op jit(solution)/shard_map/all_to_all | solution.py:403
  85.8 19.4 %copy-start.1 = (bf16[1024,2048]{1,0:T(8,128)(2,1)S(1)}, bf16[1024,2048]{1,0:T(8,128)(2,1)}, u32[]{:S(2)}) copy-start(bf16[1024,2048]{1,0:T(8,128)(2,1)} %x_ref.3) | copy-start | bytes 12582916
  86.7 18.4 %copy-start.38 = (bf16[2048,8]{0,1:T(8,128)(2,1)S(1)}, bf16[2048,8]{0,1:T(8,128)(2,1)}, u32[]{:S(2)}) copy-start(bf16[2048,8]{0,1:T(8,128)(2,1)} %param.21) | copy-start | bytes 98308
  86.8 37.7 %collective-permute-start.15 = (bf16[1472,256]{1,0:T(8,128)(2,1)}, bf16[1472,256]{1,0:T(8,128)(2,1)S(1)}, u32[]{:S(2)}, u32[]{:S(2)}) collective-permute-start(bf16[1472,256]{1,0:T(8,128)(2,1)} %slice.213), channel_id=1, source_target_pairs={{0,96},{8,104},{16,112},{24,120},{32,0},{40,8},{48,16},{56,24},{64... | collective-permute-start | bytes 2261000 | tf_op jit(solution)/shard_map/ppermute | solution.py:34
  90.6 15.8 %copy-start.36 = (s32[1024,2]{0,1:T(2,128)S(1)}, s32[1024,2]{0,1:T(2,128)}, u32[]{:S(2)}) copy-start(s32[1024,2]{0,1:T(2,128)} %param.15) | copy-start | bytes 24580
  101.7 23.1 %collective-permute-start.14 = (bf16[1472,256]{1,0:T(8,128)(2,1)}, bf16[1472,256]{1,0:T(8,128)(2,1)S(1)}, u32[]{:S(2)}, u32[]{:S(2)}) collective-permute-start(bf16[1472,256]{1,0:T(8,128)(2,1)} %slice.212), channel_id=1, source_target_pairs={{0,32},{8,40},{16,48},{24,56},{32,64},{40,72},{48,80},{56,88},{64,... | collective-permute-start | bytes 2261000 | tf_op jit(solution)/shard_map/ppermute | solution.py:34
  101.7 23.1 %collective-permute-start.7 = (bf16[1472,256]{1,0:T(8,128)(2,1)}, bf16[1472,256]{1,0:T(8,128)(2,1)S(1)}, u32[]{:S(2)}, u32[]{:S(2)}) collective-permute-start(bf16[1472,256]{1,0:T(8,128)(2,1)} %slice.202), channel_id=1, source_target_pairs={{0,24},{8,0},{16,8},{24,16},{32,56},{40,32},{48,40},{56,48},{64,88... | collective-permute-start | bytes 2261000 | tf_op jit(solution)/shard_map/ppermute | solution.py:34
  106.4 1.6 copy-start.39
  107.8 23.2 %collective-permute-start.6 = (bf16[1472,256]{1,0:T(8,128)(2,1)S(1)}, bf16[1472,256]{1,0:T(8,128)(2,1)}, u32[]{:S(2)}, u32[]{:S(2)}) collective-permute-start(bf16[1472,256]{1,0:T(8,128)(2,1)S(1)} %slice.201), channel_id=1, source_target_pairs={{0,8},{8,16},{16,24},{24,0},{32,40},{40,48},{48,56},{56,32},{64,72... | collective-permute-start | bytes 2261000 | tf_op jit(solution)/shard_map/ppermute | solution.py:34
  111.8 18.4 %copy-start.42 = (s32[64]{0:T(128)S(1)}, s32[64]{0:T(128)}, u32[]{:S(2)}) copy-start(s32[64]{0:T(128)} %param.20) | copy-start | bytes 772
  111.8 18.4 %copy-start.43 = (s32[4]{0:T(128)S(1)}, s32[4]{0:T(128)}, u32[]{:S(2)}) copy-start(s32[4]{0:T(128)} %param.19) | copy-start | bytes 52
  111.8 18.6 %copy-start.40 = (s32[4]{0:T(128)S(1)}, s32[4]{0:T(128)}, u32[]{:S(2)}) copy-start(s32[4]{0:T(128)} %param.17) | copy-start | bytes 52
  113.8 91.1 %collective-permute-start.19 = (bf16[1024,256]{1,0:T(8,128)(2,1)}, bf16[1024,256]{1,0:T(8,128)(2,1)}, u32[]{:S(2)}, u32[]{:S(2)}) collective-permute-start(bf16[1024,256]{1,0:T(8,128)(2,1)} %slice.221), channel_id=1, source_target_pairs={{0,24},{8,0},{16,8},{24,16},{32,56},{40,32},{48,40},{56,48},{64,88... | collective-permute-start | bytes 1572872 | tf_op jit(solution)/shard_map/ppermute | solution.py:34
  124.5 6.5 %copy-start.14 = (bf16[1472,256]{1,0:T(8,128)(2,1)}, bf16[1472,256]{1,0:T(8,128)(2,1)S(1)}, u32[]{:S(2)}) copy-start(bf16[1472,256]{1,0:T(8,128)(2,1)S(1)} %collective-permute-done.15.refs_9_) | copy-start | bytes 2260996
  124.5 80.3 %collective-permute-start.18 = (bf16[1024,256]{1,0:T(8,128)(2,1)}, bf16[1024,256]{1,0:T(8,128)(2,1)}, u32[]{:S(2)}, u32[]{:S(2)}) collective-permute-start(bf16[1024,256]{1,0:T(8,128)(2,1)} %slice.220), channel_id=1, source_target_pairs={{0,8},{8,16},{16,24},{24,0},{32,40},{40,48},{48,56},{56,32},{64,72... | collective-permute-start | bytes 1572872 | tf_op jit(solution)/shard_map/ppermute | solution.py:34
  124.7 6.3 %copy-start.17 = (bf16[1472,256]{1,0:T(8,128)(2,1)}, bf16[1472,256]{1,0:T(8,128)(2,1)S(1)}, u32[]{:S(2)}) copy-start(bf16[1472,256]{1,0:T(8,128)(2,1)S(1)} %collective-permute-done.14.refs_8_) | copy-start | bytes 2260996
  124.7 80.1 %collective-permute-start.23 = (bf16[1024,256]{1,0:T(8,128)(2,1)}, bf16[1024,256]{1,0:T(8,128)(2,1)}, u32[]{:S(2)}, u32[]{:S(2)}) collective-permute-start(bf16[1024,256]{1,0:T(8,128)(2,1)} %slice.223), channel_id=1, source_target_pairs={{0,96},{8,104},{16,112},{24,120},{32,0},{40,8},{48,16},{56,24},{64... | collective-permute-start | bytes 1572872 | tf_op jit(solution)/shard_map/ppermute | solution.py:34
  124.7 6.3 %copy-start.20 = (bf16[1472,256]{1,0:T(8,128)(2,1)}, bf16[1472,256]{1,0:T(8,128)(2,1)S(1)}, u32[]{:S(2)}) copy-start(bf16[1472,256]{1,0:T(8,128)(2,1)S(1)} %collective-permute-done.7.refs_4_) | copy-start | bytes 2260996
  124.8 80.1 %collective-permute-start.22 = (bf16[1024,256]{1,0:T(8,128)(2,1)}, bf16[1024,256]{1,0:T(8,128)(2,1)}, u32[]{:S(2)}, u32[]{:S(2)}) collective-permute-start(bf16[1024,256]{1,0:T(8,128)(2,1)} %slice.222), channel_id=1, source_target_pairs={{0,32},{8,40},{16,48},{24,56},{32,64},{40,72},{48,80},{56,88},{64,... | collective-permute-start | bytes 1572872 | tf_op jit(solution)/shard_map/ppermute | solution.py:34
  131.0 11.2 %copy-start.7 = (bf16[2944,256]{1,0:T(8,128)(2,1)S(1)}, bf16[2944,256]{1,0:T(8,128)(2,1)}, u32[]{:S(2)}) copy-start(bf16[2944,256]{1,0:T(8,128)(2,1)} %copy-done.6) | copy-start | bytes 4521988
  134.1 8.1 %copy-start.5 = (bf16[2944,256]{1,0:T(8,128)(2,1)S(1)}, bf16[2944,256]{1,0:T(8,128)(2,1)}, u32[]{:S(2)}) copy-start(bf16[2944,256]{1,0:T(8,128)(2,1)} %copy-done.4) | copy-start | bytes 4521988
  134.1 8.1 %copy-start.28 = (s32[13]{0:T(128)S(1)}, s32[13]{0:T(128)}, u32[]{:S(2)}) copy-start(s32[13]{0:T(128)} %pad_add_fusion.2.info_ref) | copy-start | bytes 160
  135.7 37.2 %all-to-all-start = ((bf16[8,4,16,256]{3,2,1,0:T(8,128)(2,1)}), bf16[8,4,16,256]{3,2,1,0:T(8,128)(2,1)S(1)}, u32[]{:S(2)}, u32[]{:S(2)}) async-start(bf16[8,4,16,256]{3,2,1,0:T(8,128)(2,1)} %broadcast_in_dim.2), calls=%async_computation | async-start | bytes 524288 | tf_op jit(solution)/shard_map/all_to_all | solution.py:422
  142.2 2.2 copy-start.2
  144.4 1.4 copy-start.9
  145.8 1.4 copy-start.12
  172.9 2.2 copy-start.3
  175.1 1.4 copy-start.10
  183.5 21.4 %copy-start.23 = (f32[1024,8]{1,0:T(8,128)S(1)}, f32[1024,8]{1,0:T(8,128)}, u32[]{:S(2)}) copy-start(f32[1024,8]{1,0:T(8,128)} %broadcast_multiply_fusion.gates_ref) | copy-start | bytes 98308
  214.1 9.9 %collective-permute-start.24 = (bf16[4,1024,256]{2,1,0:T(8,128)(2,1)S(1)}, bf16[4,1024,256]{2,1,0:T(8,128)(2,1)S(1)}, u32[]{:S(2)}, u32[]{:S(2)}) collective-permute-start(bf16[4,1024,256]{2,1,0:T(8,128)(2,1)S(1)} %project_out.3), channel_id=1, source_target_pairs={{0,1},{1,0},{2,3},{3,2},{4,5},{5,4},{6,7},{7,6},{8,9},{9,8},{10,11... | collective-permute-start | bytes 6291464 | tf_op jit(solution)/shard_map/ppermute | solution.py:324
  224.6 9.7 %collective-permute-start.25 = (bf16[512,256]{1,0:T(8,128)(2,1)S(1)}, bf16[512,256]{1,0:T(8,128)(2,1)S(1)}, u32[]{:S(2)}, u32[]{:S(2)}) collective-permute-start(bf16[512,256]{1,0:T(8,128)(2,1)S(1)} %get-tuple-element.11), channel_id=1, source_target_pairs={{0,2},{1,3},{2,4},{3,5},{4,6},{5,7},{6,0},{7,1},{8,10},{9,11},{10,... | collective-permute-start | bytes 786440 | tf_op jit(solution)/shard_map/ppermute | solution.py:325
  226.6 8.5 %collective-permute-start.27 = (bf16[512,256]{1,0:T(8,128)(2,1)S(1)}, bf16[512,256]{1,0:T(8,128)(2,1)S(1)}, u32[]{:S(2)}, u32[]{:S(2)}) collective-permute-start(bf16[512,256]{1,0:T(8,128)(2,1)S(1)} %get-tuple-element.12), channel_id=1, source_target_pairs={{0,6},{1,7},{2,0},{3,1},{4,2},{5,3},{6,4},{7,5},{8,14},{9,15},{10,... | collective-permute-start | bytes 786440 | tf_op jit(solution)/shard_map/ppermute | solution.py:325
  235.3 13.4 %collective-permute-start.28 = (bf16[1024,256]{1,0:T(8,128)(2,1)S(1)}, bf16[1024,256]{1,0:T(8,128)(2,1)S(1)}, u32[]{:S(2)}, u32[]{:S(2)}) collective-permute-start(bf16[1024,256]{1,0:T(8,128)(2,1)S(1)} %pad_maximum_fusion.3), channel_id=1, source_target_pairs={{0,6},{1,7},{2,0},{3,1},{4,2},{5,3},{6,4},{7,5},{8,14},{9,15},{10,... | collective-permute-start | bytes 1572872 | tf_op jit(solution)/shard_map/ppermute | solution.py:325
  237.5 13.9 %collective-permute-start.26 = (bf16[1024,256]{1,0:T(8,128)(2,1)S(1)}, bf16[1024,256]{1,0:T(8,128)(2,1)S(1)}, u32[]{:S(2)}, u32[]{:S(2)}) collective-permute-start(bf16[1024,256]{1,0:T(8,128)(2,1)S(1)} %pad_maximum_fusion.2), channel_id=1, source_target_pairs={{0,2},{1,3},{2,4},{3,5},{4,6},{5,7},{6,0},{7,1},{8,10},{9,11},{10,... | collective-permute-start | bytes 1572872 | tf_op jit(solution)/shard_map/ppermute | solution.py:325
  (16 other events, 17.2 us)
